TPU v7x, 32 devices: a whole 2x2x4 slice. The times are simulated.
32 devices in a mesh: groups: 2 (over y), ctx: 4 (over z), head: 2 (over x), dp: 2 (over core).
Axes of the slice: x: 2, y: 2, z: 4, core: 2. Of those that a mesh axis runs over, the one named last changes fastest.
Arguments:
- query_input: bfloat16 [4, 512, 16, 128], P(('groups', 'dp'), 'ctx', 'head'), parts along dimension 0, may hold values from -6 to 6
- key_input: bfloat16 [4, 512, 3, 16, 128], P(('groups', 'dp'), 'ctx', None, 'head'), parts along dimension 0, may hold values from -6 to 6
- value_input: bfloat16 [4, 512, 3, 16, 128], P(('groups', 'dp'), 'ctx', None, 'head'), parts along dimension 0, may hold values from -6 to 6
- beta_logit: float32 [4, 16, 3, 512], P(('groups', 'dp'), 'head', None, 'ctx'), parts along dimension 0, may hold values from -6 to 6
- gate_logit: float32 [4, 16, 512], P(('groups', 'dp'), 'head', 'ctx'), parts along dimension 0, may hold values from -6 to 1536
- decay_rate: float32 [16], P('head'), may hold values from 0.00048828125 to 0.05
- doc_ids: int32 [4, 8], P(('groups', 'dp')), parts along dimension 0, may hold values from 0 to 1, never falling along the last dimension, each value on 1 to 7 neighbouring positions
- out_weight: bfloat16 [2048, 2048], P('head'), may hold values from -0.125 to 0.125
- out_cotangent: bfloat16 [4, 512, 2048], P(('groups', 'dp'), 'ctx'), parts along dimension 0, may hold values from -6 to 6
Outputs:
- mixed: bfloat16 [4, 512, 2048], P(('groups', 'dp'), 'ctx', 'head'), parts along dimension 0
- query_grad: bfloat16 [4, 512, 16, 128], P(('groups', 'dp'), 'ctx', 'head'), parts along dimension 0
- key_grad: bfloat16 [4, 512, 3, 16, 128], P(('groups', 'dp'), 'ctx', None, 'head'), parts along dimension 0
- value_grad: bfloat16 [4, 512, 3, 16, 128], P(('groups', 'dp'), 'ctx', None, 'head'), parts along dimension 0
- beta_grad: float32 [4, 16, 3, 512], P(('groups', 'dp'), 'head', None, 'ctx'), parts along dimension 0
- gate_grad: float32 [4, 16, 512], P(('groups', 'dp'), 'head', 'ctx'), parts along dimension 0
- weight_grad: float32 [4096, 2048], P(('groups', 'ctx'), 'head'), parts along dimension 0
- rate_grad: float32 [32], P(('groups', 'head')), parts along dimension 0
There are 2 independent parts, one for each index of `groups`. A program takes and returns all parts, laid end to end along the dimension named above; an argument that names none is the same for every part. Nothing has to cross between parts.
Inputs may be any that keep to these rules, and one draw needn't show every extreme that they name: `doc_ids`: in each sequence the numbers never fall along the stretches, every number of 0 to 1 appears, each covers 1 to 7 stretches.
All inputs are finite; a program needn't handle non-finite values.
Results may differ from a plain program's by a relative error of at most 0.0051.
Values sent between devices are 32-bit elements; how exact they have to be, the bound alone decides.
A program may use at most 192 MiB of HBM per device.

v0:
```python
import jax
import jax.numpy as jnp
from jax import lax
from jax.sharding import PartitionSpec as P

CH = 64
NF = 3


def shifted(value, axis, steps):
    count = lax.axis_size(axis)
    first, last = (max(0, -steps), min(count, count - steps))
    return lax.ppermute(value, axis, [(source, source + steps) for source in range(first, last)])


def prepare(query_input, key_input, value_input, beta_logit, gate_logit, decay_rate):
    seq_count, length, head_count, key_width = query_input.shape
    value_width = value_input.shape[-1]
    batch = seq_count * head_count
    blocks = length // CH
    span = CH * NF
    query = (
        (query_input * key_width ** (-0.5))
        .transpose(0, 2, 1, 3)
        .reshape(batch, blocks, CH, key_width)
    )
    squares = jnp.sum(key_input * key_input, axis=-1, keepdims=True)
    keys = (
        (key_input * lax.rsqrt(squares + 1e-06))
        .transpose(0, 3, 1, 2, 4)
        .reshape(batch, blocks, span, key_width)
    )
    values = value_input.transpose(0, 3, 1, 2, 4).reshape(batch, blocks, span, value_width)
    betas = (2.0 * jax.nn.sigmoid(beta_logit)).transpose(0, 1, 3, 2).reshape(batch, blocks, span)
    log_decay = -decay_rate[None, :, None] * jax.nn.softplus(gate_logit)
    spread = jnp.concatenate(
        [log_decay[..., None], jnp.zeros(log_decay.shape + (NF - 1,), log_decay.dtype)], axis=-1
    )
    cumulative = jnp.cumsum(spread.reshape(batch, blocks, span), axis=-1)
    return tuple((jnp.moveaxis(piece, 1, 0) for piece in (query, keys, values, betas, cumulative)))


def stretch_step(carry_state, pieces):
    query_block, key_block, value_block, beta_block, cumul_block, retain_block = pieces
    highest_level = lax.Precision.HIGHEST
    value_width = value_block.shape[-1]
    total_width = carry_state.shape[-1]
    span = key_block.shape[1]
    entry = carry_state * retain_block[:, None, None]
    token_indices = jnp.arange(span)
    strict = token_indices[:, None] > token_indices[None, :]
    gap = cumul_block[:, :, None] - cumul_block[:, None, :]
    decay_pairs = jnp.exp(jnp.where(strict, gap, 0.0)) * strict
    key_gram = jnp.einsum("nid,njd->nij", key_block, key_block, precision=highest_level)
    lower_factor = (
        jnp.eye(span, dtype=key_gram.dtype) + beta_block[:, :, None] * decay_pairs * key_gram
    )
    growth = jnp.exp(cumul_block)
    right_side = (
        jnp.concatenate([value_block, growth[..., None] * key_block], axis=-1)
        * beta_block[..., None]
    )
    solved = jax.scipy.linalg.solve_triangular(
        lower_factor, right_side, lower=True, unit_diagonal=True
    )
    updates = jnp.pad(solved[..., :value_width], ((0, 0), (0, 0), (0, total_width - value_width)))
    correction = updates - jnp.einsum(
        "nmk,nke->nme", solved[..., value_width:], entry, precision=highest_level
    )
    read_index = token_indices[NF - 1 :: NF]
    read_cumul = cumul_block[:, NF - 1 :: NF]
    visible = token_indices[None, :] <= read_index[:, None]
    read_gap = read_cumul[:, :, None] - cumul_block[:, None, :]
    read_decay = jnp.exp(jnp.where(visible, read_gap, 0.0)) * visible
    query_key = jnp.einsum("ntd,njd->ntj", query_block, key_block, precision=highest_level)
    outputs = jnp.exp(read_cumul)[..., None] * jnp.einsum(
        "ntd,nde->nte", query_block, entry, precision=highest_level
    )
    outputs = outputs + jnp.einsum(
        "ntj,nje->nte", query_key * read_decay, correction, precision=highest_level
    )
    last_cumul = cumul_block[:, -1]
    scaled_keys = jnp.exp(last_cumul[:, None] - cumul_block)[..., None] * key_block
    advanced = jnp.exp(last_cumul)[:, None, None] * entry + jnp.einsum(
        "njd,nje->nde", scaled_keys, correction, precision=highest_level
    )
    return (advanced, outputs)


def apply_map(transition_matrix, state_vector, start_offset):
    return (
        jnp.einsum("swa,sag->swg", transition_matrix, state_vector, precision=lax.Precision.HIGHEST)
        + start_offset
    )


def on_device(
    query_input,
    key_input,
    value_input,
    beta_logit,
    gate_logit,
    decay_rate,
    doc_ids,
    out_weight,
    out_cotangent,
):
    highest_level = lax.Precision.HIGHEST
    seq_count, length, head_count, key_width = query_input.shape
    value_width = value_input.shape[-1]
    model_width = out_cotangent.shape[-1]
    batch = seq_count * head_count
    blocks = length // CH
    ctx_size = lax.axis_size("ctx")
    padded = jnp.concatenate([jnp.full((seq_count, 1), -1, jnp.int32), doc_ids], axis=1)
    window = lax.dynamic_slice_in_dim(padded, lax.axis_index("ctx") * blocks, blocks + 1, 1)
    retain = jnp.repeat((window[:, 1:] == window[:, :-1]).astype(jnp.float32), head_count, axis=0)
    anchor = jnp.concatenate(
        [
            jnp.zeros((batch, key_width, value_width), jnp.float32),
            jnp.broadcast_to(jnp.eye(key_width, dtype=jnp.float32), (batch, key_width, key_width)),
        ],
        axis=-1,
    )

    def local_pass(query, keys, values, betas, gates, rates):
        pieces = prepare(query, keys, values, betas, gates, rates) + (jnp.moveaxis(retain, 1, 0),)
        closing, outputs = lax.scan(stretch_step, anchor, pieces)
        return (
            jnp.moveaxis(outputs, 0, 1).reshape(batch, length, value_width + key_width),
            closing,
        )

    (outputs, closing), pullback = jax.vjp(
        local_pass,
        query_input.astype(jnp.float32),
        key_input.astype(jnp.float32),
        value_input.astype(jnp.float32),
        beta_logit,
        gate_logit,
        decay_rate,
    )
    local_core_state = outputs[..., :value_width]
    route_paths = outputs[..., value_width:]
    start_offset = closing[..., :value_width]
    transfer = closing[..., value_width:]
    state_zeros = jnp.zeros((batch, key_width, value_width), jnp.float32)

    def forward_turn(turn, incoming_state):
        return shifted(apply_map(transfer, incoming_state, start_offset), "ctx", 1)

    incoming_state = lax.fori_loop(0, ctx_size - 1, forward_turn, state_zeros)
    core_state = local_core_state + jnp.einsum(
        "uwb,ubr->uwr", route_paths, incoming_state, precision=highest_level
    )
    core_rows = core_state.reshape(seq_count, head_count, length, value_width).transpose(0, 2, 1, 3)
    core_rows = core_rows.reshape(seq_count * length, head_count * value_width).astype(jnp.bfloat16)
    partial_out = jnp.dot(core_rows, out_weight, preferred_element_type=jnp.float32).reshape(
        seq_count, length, model_width
    )
    mixed = lax.psum_scatter(partial_out, "head", scatter_dimension=2, tiled=True).astype(
        jnp.bfloat16
    )
    cot_rows = out_cotangent.reshape(seq_count * length, model_width)
    core_state_grad = jnp.dot(cot_rows, out_weight.T, preferred_element_type=jnp.float32)
    core_state_grad = (
        core_state_grad.reshape(seq_count, length, head_count, value_width)
        .transpose(0, 2, 1, 3)
        .reshape(batch, length, value_width)
    )
    local_gradient = jnp.einsum(
        "jhu,jhf->juf", route_paths, core_state_grad, precision=highest_level
    )
    transposed = jnp.swapaxes(transfer, 1, 2)

    def backward_turn(turn, outgoing_state):
        return shifted(apply_map(transposed, outgoing_state, local_gradient), "ctx", -1)

    outgoing_state = lax.fori_loop(0, ctx_size - 1, backward_turn, state_zeros)
    adjoint_results = jnp.concatenate(
        [
            core_state_grad,
            jnp.einsum("icu,iou->ico", core_state_grad, incoming_state, precision=highest_level),
        ],
        axis=-1,
    )
    adjoint_final = jnp.concatenate(
        [
            outgoing_state,
            jnp.einsum("cip,crp->cir", outgoing_state, incoming_state, precision=highest_level),
        ],
        axis=-1,
    )
    gradients = pullback((adjoint_results, adjoint_final))
    portion = lax.psum_scatter(
        jnp.einsum("td,te->de", cot_rows, core_rows, preferred_element_type=jnp.float32),
        "ctx",
        scatter_dimension=0,
        tiled=True,
    )
    weight_grad = lax.psum(portion, "dp")
    rate_grad = lax.psum(gradients[5], ("ctx", "dp"))
    return (
        mixed,
        gradients[0].astype(jnp.bfloat16),
        gradients[1].astype(jnp.bfloat16),
        gradients[2].astype(jnp.bfloat16),
        gradients[3],
        gradients[4],
        weight_grad,
        rate_grad,
    )


def solution(mesh):
    in_specs = (
        P(("groups", "dp"), "ctx", "head", None),
        P(("groups", "dp"), "ctx", None, "head", None),
        P(("groups", "dp"), "ctx", None, "head", None),
        P(("groups", "dp"), "head", None, "ctx"),
        P(("groups", "dp"), "head", "ctx"),
        P("head"),
        P(("groups", "dp"), None),
        P("head", None),
        P(("groups", "dp"), "ctx", None),
    )
    out_specs = (
        P(("groups", "dp"), "ctx", "head"),
        P(("groups", "dp"), "ctx", "head", None),
        P(("groups", "dp"), "ctx", None, "head", None),
        P(("groups", "dp"), "ctx", None, "head", None),
        P(("groups", "dp"), "head", None, "ctx"),
        P(("groups", "dp"), "head", "ctx"),
        P(("groups", "ctx"), "head"),
        P(("groups", "head")),
    )
    return jax.shard_map(
        on_device, mesh=mesh, in_specs=in_specs, out_specs=out_specs, check_vma=False
    )
```

profile of v0, /device:TPU:0, one launch (start us, length us, event | category | flops | bytes accessed | tf_op | source)
XLA Modules:
  0.0 1163.1 jit_solution(5929489049513144267)
XLA Ops:
  26.6 416.6 %while.124 = (s32[]{:T(128)}, f32[8,128,256]{2,1,0:T(8,128)S(1)}, f32[2,8,64,256]{3,2,1,0:T(8,128)}, f32[2,8,1,1]{1,3,2,0:T(1,128)}, f32[2,8,192,192]{3,2,1,0:T(...) while((s32[]{:T(128)}, f32[8,128,256]{2,1,0:T(8,128)S(1)}, ...), condition=%wide.region_4.5_spmd.clone.clone, body=%wide.region_3.4_spmd.clone.clone.sunk | while | flops 3032945408 | bytes 259570128 | solution.py:128
  29.1 5.3 select_add_fusion.5
  36.6 158.6 %custom-call.52 = f32[8,2,128,128]{2,3,1,0:T(8,128)} custom-call(f32[8,2,128,128]{3,2,1,0:T(8,128)} %pad_maximum_fusion.11), custom_call_target="InvertDiagBlocksLowerTriangular" | custom-call | tf_op jit(solution)/shard_map/jvp()/while/body/eval_jaxpr/jit(_solve_triangular)/vmap()/triangular_solve | solution.py:63
  213.4 4.1 bitcast_dynamic-update-slice_fusion.20
  236.9 5.3 select_add_fusion.5
  244.4 158.6 %custom-call.52 = f32[8,2,128,128]{2,3,1,0:T(8,128)} custom-call(f32[8,2,128,128]{3,2,1,0:T(8,128)} %pad_maximum_fusion.11), custom_call_target="InvertDiagBlocksLowerTriangular" | custom-call | tf_op jit(solution)/shard_map/jvp()/while/body/eval_jaxpr/jit(_solve_triangular)/vmap()/triangular_solve | solution.py:63
  421.3 4.1 bitcast_dynamic-update-slice_fusion.20
  446.8 50.1 %while.121 = (s32[]{:T(128)}, f32[8,128,128]{2,1,0:T(8,128)S(1)}, f32[8,128,128]{2,1,0:T(8,128)}, f32[8,128,128]{2,1,0:T(8,128)}, s32[]{:T(128)}) while((s32[]{:T(128)}, f32[8,128,128]{2,1,0:T(8,128)S(1)}, f32[8,128,128]{2,1,0:T(8,128)}, f32[8,128,128]{2,1,0:T(8,128)}, s32[]{:T(128)}) %tuple.231), condition=%wide.region_6.7_spmd, body=%wide.region_5.6_spmd.sunk | while | flops 201457664 | bytes 4194405 | solution.py:152
  448.7 5.0 collective-permute-start
  453.7 11.1 collective-permute-done
  466.7 4.4 collective-permute-start
  471.1 10.3 collective-permute-done
  483.2 4.4 collective-permute-start
  487.6 9.3 collective-permute-done
  499.0 4.6 convolution_bitcast_fusion
  503.7 3.9 convolution_bitcast_fusion.1
  507.7 3.8 fusion.193
  514.4 124.8 %while.122 = (s32[]{:T(128)}, f32[8,128,128]{2,1,0:T(8,128)S(1)}, f32[8,128,128]{2,1,0:T(8,128)}, f32[8,128,128]{2,1,0:T(8,128)S(1)}, s32[]{:T(128)}) while((s32[]{:T(128)}, f32[8,128,128]{2,1,0:T(8,128)S(1)}, f32[8,128,128]{2,1,0:T(8,128)}, f32[8,128,128]{2,1,0:T(8,128)S(1)}, s32[]{:T(128)}) %tuple.234), condition=%wide.region_9.10_spmd, body=%wide.region_8.9_spmd.sunk | while | flops 201457664 | bytes 4194405 | solution.py:179
  518.2 36.5 %collective-permute-done.1 = f32[8,128,128]{2,1,0:T(8,128)S(1)} collective-permute-done((f32[8,128,128]{2,1,0:T(8,128)}, f32[8,128,128]{2,1,0:T(8,128)S(1)}, u32[]{:S(2)}, u32[]{:S(2)}) %collective-permute-start.1) | collective-permute-done | bytes 524320 | tf_op jit(solution)/shard_map/while/body/eval_jaxpr/ppermute | solution.py:13
  558.5 40.0 %collective-permute-done.1 = f32[8,128,128]{2,1,0:T(8,128)S(1)} collective-permute-done((f32[8,128,128]{2,1,0:T(8,128)}, f32[8,128,128]{2,1,0:T(8,128)S(1)}, u32[]{:S(2)}, u32[]{:S(2)}) %collective-permute-start.1) | collective-permute-done | bytes 524320 | tf_op jit(solution)/shard_map/while/body/eval_jaxpr/ppermute | solution.py:13
  602.3 36.9 %collective-permute-done.1 = f32[8,128,128]{2,1,0:T(8,128)S(1)} collective-permute-done((f32[8,128,128]{2,1,0:T(8,128)}, f32[8,128,128]{2,1,0:T(8,128)S(1)}, u32[]{:S(2)}, u32[]{:S(2)}) %collective-permute-start.1) | collective-permute-done | bytes 524320 | tf_op jit(solution)/shard_map/while/body/eval_jaxpr/ppermute | solution.py:13
  652.5 467.5 %while.123 = (s32[]{:T(128)}, f32[8,128,256]{2,1,0:T(8,128)S(1)}, f32[2,8,64,128]{3,2,1,0:T(8,128)}, f32[2,8,192,128]{3,2,1,0:T(8,128)}, bf16[2,8,192,128]{3,2,1...) while((s32[]{:T(128)}, f32[8,128,256]{2,1,0:T(8,128)S(1)}, ...), condition=%wide.region_22.23_spmd.clone, body=%wide.region_10.22_spmd.clone.sunk | while | flops 6785894912 | bytes 272479616 | solution.py:128
  687.9 158.6 %custom-call.51 = f32[8,2,128,128]{2,3,1,0:T(8,128)} custom-call(f32[8,2,128,128]{3,2,1,0:T(8,128)} %pad_maximum_fusion.10), custom_call_target="InvertDiagBlocksLowerTriangular" | custom-call | tf_op jit(solution)/shard_map/transpose(jvp())/while/body/eval_jaxpr/jit(_solve_triangular)/vmap()/triangular_solve | solution.py:63
  857.6 3.4 fusion.362
  872.4 4.4 fusion.342
  877.2 5.0 fusion.353
  908.8 158.6 %custom-call.51 = f32[8,2,128,128]{2,3,1,0:T(8,128)} custom-call(f32[8,2,128,128]{3,2,1,0:T(8,128)} %pad_maximum_fusion.10), custom_call_target="InvertDiagBlocksLowerTriangular" | custom-call | tf_op jit(solution)/shard_map/transpose(jvp())/while/body/eval_jaxpr/jit(_solve_triangular)/vmap()/triangular_solve | solution.py:63
  1078.4 3.4 fusion.362
  1093.2 4.4 fusion.342
  1098.0 5.0 fusion.353
  1120.1 5.0 reduce-window.16
  1125.9 14.5 %psum.15 = f32[8]{0:T(128)} all-reduce(f32[8]{0:T(128)S(1)} %neg.57), channel_id=1, replica_groups=mesh['groups'=2,'ctx'=4,'head'=2,'dp'=2] {'ctx','dp'}, use_global_device_ids=true, to_apply=%region_29.30 | all-reduce | flops 8 | bytes 64 | tf_op jit(solution)/shard_map/psum | solution.py:202
  (740 shorter events, 250.4 us)
Async XLA Ops:
  7.2 491.8 %copy-start = (bf16[1,128,2048]{2,1,0:T(8,128)(2,1)S(1)}, bf16[1,128,2048]{2,1,0:T(8,128)(2,1)}, u32[]{:S(2)}) copy-start(bf16[1,128,2048]{2,1,0:T(8,128)(2,1)} %param.25) | copy-start | bytes 1572868
  7.2 1118.0 %reduce-scatter.5.cloned.1.call-start = ((), (), s32[]{:S(2)}) async-start(), calls=%async_computation.3 | async-start | bytes 10485760 | tf_op jit(solution)/shard_map/reduce_scatter | solution.py:195
  28.9 167.9 %copy-start.66 = (f32[8,192]{1,0:T(8,128)}, f32[8,192]{1,0:T(8,128)S(1)}, u32[]{:S(2)}) copy-start(f32[8,192]{1,0:T(8,128)S(1)} %fusion.376) | copy-start | bytes 18436 | tf_op jit(solution)/shard_map/jvp()/while
  202.1 8.7 copy-start.33
  202.9 7.9 copy-start.75
  213.4 11.1 copy-start.38
  224.6 7.7 copy-start.91
  224.6 7.7 copy-start.114
  224.7 7.7 copy-start.115
  224.7 7.7 copy-start.118
  224.7 7.7 copy-start.108
  224.7 7.7 copy-start.105
  236.8 167.9 %copy-start.66 = (f32[8,192]{1,0:T(8,128)}, f32[8,192]{1,0:T(8,128)S(1)}, u32[]{:S(2)}) copy-start(f32[8,192]{1,0:T(8,128)S(1)} %fusion.376) | copy-start | bytes 18436 | tf_op jit(solution)/shard_map/jvp()/while
  410.0 8.7 copy-start.33
  410.8 7.9 copy-start.75
  421.3 11.2 copy-start.38
  432.6 7.7 copy-start.91
  432.6 7.7 copy-start.114
  432.6 7.7 copy-start.115
  432.6 7.7 copy-start.118
  432.6 7.8 copy-start.108
  432.6 7.8 copy-start.105
  448.7 16.1 %collective-permute-start = (f32[8,128,128]{2,1,0:T(8,128)S(1)}, f32[8,128,128]{2,1,0:T(8,128)S(1)}, u32[]{:S(2)}, u32[]{:S(2)}) collective-permute-start(f32[8,128,128]{2,1,0:T(8,128)S(1)} %convolution_add_fusion.13), channel_id=1, source_target_pairs={{0,4},{4,8},{8,12},{1,5},{5,9},{9,13},{2,6},{6,10},{10,14},{3,7},{... | collective-permute-start | bytes 1572872 | tf_op jit(solution)/shard_map/while/body/eval_jaxpr/ppermute | solution.py:13
  466.7 14.7 %collective-permute-start = (f32[8,128,128]{2,1,0:T(8,128)S(1)}, f32[8,128,128]{2,1,0:T(8,128)S(1)}, u32[]{:S(2)}, u32[]{:S(2)}) collective-permute-start(f32[8,128,128]{2,1,0:T(8,128)S(1)} %convolution_add_fusion.13), channel_id=1, source_target_pairs={{0,4},{4,8},{8,12},{1,5},{5,9},{9,13},{2,6},{6,10},{10,14},{3,7},{... | collective-permute-start | bytes 1572872 | tf_op jit(solution)/shard_map/while/body/eval_jaxpr/ppermute | solution.py:13
  483.2 13.8 %collective-permute-start = (f32[8,128,128]{2,1,0:T(8,128)S(1)}, f32[8,128,128]{2,1,0:T(8,128)S(1)}, u32[]{:S(2)}, u32[]{:S(2)}) collective-permute-start(f32[8,128,128]{2,1,0:T(8,128)S(1)} %convolution_add_fusion.13), channel_id=1, source_target_pairs={{0,4},{4,8},{8,12},{1,5},{5,9},{9,13},{2,6},{6,10},{10,14},{3,7},{... | collective-permute-start | bytes 1572872 | tf_op jit(solution)/shard_map/while/body/eval_jaxpr/ppermute | solution.py:13
  503.6 648.0 %reduce-scatter.3.cloned.1.call-start = ((), (), s32[]{:S(2)}) async-start(), calls=%async_computation.2 | async-start | bytes 1572864 | tf_op jit(solution)/shard_map/reduce_scatter | solution.py:161
  507.6 645.9 %all-reduce.13.cloned.1.call-start = ((), (), s32[]{:S(2)}) async-start(), calls=%async_computation.4 | async-start | bytes 4194304 | tf_op jit(solution)/shard_map/psum | solution.py:201
  516.9 37.8 %collective-permute-start.1 = (f32[8,128,128]{2,1,0:T(8,128)}, f32[8,128,128]{2,1,0:T(8,128)S(1)}, u32[]{:S(2)}, u32[]{:S(2)}) collective-permute-start(f32[8,128,128]{2,1,0:T(8,128)} %convolution_add_fusion.14), channel_id=1, source_target_pairs={{4,0},{8,4},{12,8},{5,1},{9,5},{13,9},{6,2},{10,6},{14,10},{7,3},{... | collective-permute-start | bytes 1572872 | tf_op jit(solution)/shard_map/while/body/eval_jaxpr/ppermute | solution.py:13
  557.2 41.3 %collective-permute-start.1 = (f32[8,128,128]{2,1,0:T(8,128)}, f32[8,128,128]{2,1,0:T(8,128)S(1)}, u32[]{:S(2)}, u32[]{:S(2)}) collective-permute-start(f32[8,128,128]{2,1,0:T(8,128)} %convolution_add_fusion.14), channel_id=1, source_target_pairs={{4,0},{8,4},{12,8},{5,1},{9,5},{13,9},{6,2},{10,6},{14,10},{7,3},{... | collective-permute-start | bytes 1572872 | tf_op jit(solution)/shard_map/while/body/eval_jaxpr/ppermute | solution.py:13
  601.0 38.2 %collective-permute-start.1 = (f32[8,128,128]{2,1,0:T(8,128)}, f32[8,128,128]{2,1,0:T(8,128)S(1)}, u32[]{:S(2)}, u32[]{:S(2)}) collective-permute-start(f32[8,128,128]{2,1,0:T(8,128)} %convolution_add_fusion.14), channel_id=1, source_target_pairs={{4,0},{8,4},{12,8},{5,1},{9,5},{13,9},{6,2},{10,6},{14,10},{7,3},{... | collective-permute-start | bytes 1572872 | tf_op jit(solution)/shard_map/while/body/eval_jaxpr/ppermute | solution.py:13
  877.2 8.4 copy-start.63
  1098.0 8.4 copy-start.63
  (187 other events, 532.6 us)
Sparse Core Ops, SparseCore 0:
  503.7 180.1 reduce-scatter.4
  686.2 20.9 reduce-scatter.2
  1125.4 22.8 all-reduce.12
where the time goes:
time: 1170 us; the launch traced here: 1160 us
  other arithmetic  693 us (59%)
  matrix products  158 us (14%)
  waiting for transfers between devices  144 us (12%)
  local copies, waits for them, and re-layouts  91.8 us (8%)
  loops' own time  29.3 us (3%)
  starting transfers between devices  17.8 us (2%)
  between operations  14.8 us (1%)
  blocking collectives  14.5 us (1%)
    another operation x34, other arithmetic, stretch_step(): jax.scipy.linalg.solve_triangular(lower_factor, right_side, lower=True, u...  641 us
    ppermute x6, waiting for transfers between devices, shifted(): lax.ppermute(value, axis, [(source, source + steps) for source in range(f...  144 us
    while x342, local copies, waits for them, and re-layouts  45.4 us
    another operation x2, loops' own time, local_pass(): closing, outputs = lax.scan(stretch_step, anchor, pieces)  29.1 us
    dot_general x6, matrix products, stretch_step(): jnp.einsum('nid,njd->nij', key_block, key_block, precision=highest_level)  27.2 us
    another operation x18, matrix products, stretch_step(): jax.scipy.linalg.solve_triangular(lower_factor, right_side, lower=True, u...  27 us
  transfers between devices with their start and end apart: 9, of which 6 were waited for; matrix products, arithmetic and copies ran while one was open for 41% of the time, Pallas kernels for 0%

commit v1 on v0

v1 whole, which is shorter than its diff:
```python
import functools

import jax
import jax.numpy as jnp
from jax import lax
from jax.experimental import pallas as pl
from jax.experimental.pallas import tpu as pltpu
from jax.sharding import PartitionSpec as P

CH = 64
NF = 3
SPAN = CH * NF
F32 = jnp.float32
BF16 = jnp.bfloat16


def mm(a, b, ta=False, tb=False, passes=1):
    dims = (((0 if ta else 1,), (1 if tb else 0,)), ((), ()))

    def one(x, y):
        return lax.dot_general(x, y, dims, preferred_element_type=F32)

    a_high, b_high = a.astype(BF16), b.astype(BF16)
    result = one(a_high, b_high)
    if passes == 3:
        a_low = (a - a_high.astype(F32)).astype(BF16)
        b_low = (b - b_high.astype(F32)).astype(BF16)
        result = result + one(a_high, b_low) + one(a_low, b_high)
    return result


def order_masks():
    row = lax.broadcasted_iota(jnp.int32, (SPAN, SPAN), 0)
    column = lax.broadcasted_iota(jnp.int32, (SPAN, SPAN), 1)
    row_time = (row % CH) * NF + row // CH
    column_time = (column % CH) * NF + column // CH
    return row_time > column_time, row_time ^ column_time


def load_stretch(s, q_ref, k_refs, v_refs, cols_ref, rows_ref):
    at = slice(s * CH, (s + 1) * CH)
    q = q_ref[at, :].astype(F32) * (q_ref.shape[-1] ** (-0.5))
    raw = jnp.concatenate([ref[at, :] for ref in k_refs], axis=0).astype(F32)
    v = jnp.concatenate([ref[at, :] for ref in v_refs], axis=0).astype(F32)
    inverse_norm = lax.rsqrt(jnp.sum(raw * raw, axis=1, keepdims=True) + 1e-06)
    k = raw * inverse_norm
    cols = cols_ref[0, at, :]
    beta = jnp.concatenate([cols[:, f : f + 1] for f in range(NF)], axis=0)
    token_cumul = cols[:, 3:4]
    token_last = cols[CH - 1 : CH, 3:4]
    cumul_row = rows_ref[0, 0:1, at]
    i = lax.broadcasted_iota(jnp.int32, (CH, CH), 0)
    j = lax.broadcasted_iota(jnp.int32, (CH, CH), 1)
    decay = jnp.where(i >= j, jnp.exp(jnp.where(i >= j, token_cumul - cumul_row, 0.0)), 0.0)
    read_decay = jnp.concatenate([decay] * NF, axis=1)
    growth = jnp.exp(token_cumul)
    tail = jnp.exp(token_last - token_cumul)
    return dict(
        q=q,
        k=k,
        v=v,
        inverse_norm=inverse_norm,
        beta=beta,
        read_decay=read_decay,
        pair_decay=jnp.concatenate([read_decay] * NF, axis=0),
        read_growth=growth,
        growth=jnp.concatenate([growth] * NF, axis=0),
        tail=jnp.concatenate([tail] * NF, axis=0),
        last=jnp.exp(token_last),
    )


def maps_kernel(
    passes, retain_ref, q_ref, k0, k1, k2, v0, v1, v2, cols_ref, rows_ref, grad_ref,
    inverse_ref, map_ref, offset_ref, pull_ref, total_map_ref, total_offset_ref, total_pull_ref,
):
    strict, differing = order_masks()
    width = q_ref.shape[-1]
    count = q_ref.shape[0] // CH
    diagonal = (
        lax.broadcasted_iota(jnp.int32, (width, width), 0)
        == lax.broadcasted_iota(jnp.int32, (width, width), 1)
    )
    parts = [load_stretch(s, q_ref, (k0, k1, k2), (v0, v1, v2), cols_ref, rows_ref) for s in range(count)]
    lowers, inverses = [], []
    for part in parts:
        gram = mm(part["k"], part["k"], tb=True, passes=passes)
        lower = jnp.where(strict, part["beta"] * part["pair_decay"] * gram, 0.0)
        lowers.append(lower)
        inverses.append(
            jnp.where(differing == 0, 1.0, 0.0) - jnp.where(differing == 1, lower, 0.0)
        )
    for level in range(1, (SPAN - 1).bit_length()):
        here = (differing >> level) == 1
        halves = [mm(jnp.where(here, low, 0.0), inv, passes=passes) for low, inv in zip(lowers, inverses)]
        inverses = [inv - mm(inv, half, passes=passes) for inv, half in zip(inverses, halves)]
    maps, offsets, pulls = [], [], []
    for s, (part, inverse) in enumerate(zip(parts, inverses)):
        inverse_ref[0, s] = inverse
        right = part["beta"] * jnp.concatenate([part["v"], part["growth"] * part["k"]], axis=1)
        solved = mm(inverse, right, passes=passes)
        moved = mm(part["tail"] * part["k"], solved, ta=True, passes=passes)
        offsets.append(moved[:, :width])
        maps.append(jnp.where(diagonal, part["last"], 0.0) - moved[:, width:])
        reads = mm(part["q"], part["k"], tb=True, passes=passes) * part["read_decay"]
        route = part["read_growth"] * part["q"] - mm(reads, solved[:, width:], passes=passes)
        pulls.append(mm(route, grad_ref[s * CH : (s + 1) * CH, :], ta=True, passes=passes))
        map_ref[0, s] = maps[-1]
        offset_ref[0, s] = offsets[-1]
        pull_ref[0, s] = pulls[-1]
    total_map, total_offset = retain_ref[0] * maps[0], offsets[0]
    for s in range(1, count):
        kept = retain_ref[s] * maps[s]
        total_map = mm(kept, total_map, passes=3)
        total_offset = mm(kept, total_offset, passes=3) + offsets[s]
    total_pull = retain_ref[count - 1] * pulls[-1]
    for s in range(count - 2, -1, -1):
        total_pull = retain_ref[s] * (pulls[s] + mm(maps[s], total_pull, ta=True, passes=3))
    total_map_ref[0] = total_map
    total_offset_ref[0] = total_offset
    total_pull_ref[0] = total_pull


def results_kernel(
    passes, retain_ref, q_ref, k0, k1, k2, v0, v1, v2, cols_ref, rows_ref, grad_ref,
    inverse_ref, map_ref, offset_ref, pull_ref, enter_ref, leave_ref,
    core_ref, dq_ref, dk0, dk1, dk2, dv0, dv1, dv2, col_out_ref, row_out_ref,
):
    strict, _ = order_masks()
    width = q_ref.shape[-1]
    count = q_ref.shape[0] // CH
    entries = [retain_ref[0] * enter_ref[0]]
    for s in range(1, count):
        entries.append(
            retain_ref[s] * (mm(map_ref[0, s - 1], entries[-1], passes=passes) + offset_ref[0, s - 1])
        )
    exits = [leave_ref[0]]
    for s in range(count - 1, 0, -1):
        exits.insert(
            0, retain_ref[s] * (mm(map_ref[0, s], exits[0], ta=True, passes=passes) + pull_ref[0, s])
        )
    mul = functools.partial(mm, passes=passes)
    for s in range(count):
        at = slice(s * CH, (s + 1) * CH)
        part = load_stretch(s, q_ref, (k0, k1, k2), (v0, v1, v2), cols_ref, rows_ref)
        q, k, beta, growth, tail = part["q"], part["k"], part["beta"], part["growth"], part["tail"]
        entry, leaving, grad = entries[s], exits[s], grad_ref[at, :]
        inverse = inverse_ref[0, s]
        gram = mul(k, k, tb=True)
        pair_decay = jnp.where(strict, part["pair_decay"], 0.0)
        on_entry = mul(jnp.concatenate([k, q], axis=0), entry)
        key_entry, query_entry = on_entry[:SPAN], on_entry[SPAN:]
        rest = part["v"] - growth * key_entry
        correction = mul(inverse, beta * rest)
        reads = mul(q, k, tb=True) * part["read_decay"]
        core_ref[at, :] = (part["read_growth"] * query_entry + mul(reads, correction)).astype(BF16)
        correction_grad = mul(reads, grad, ta=True) + tail * mul(k, leaving)
        right_grad = mul(inverse, correction_grad, ta=True)
        rest_grad = beta * right_grad
        outer = mul(jnp.concatenate([right_grad, grad], axis=0), correction, tb=True)
        scaled = -outer[:SPAN] * pair_decay
        reads_grad = outer[SPAN:]
        paired = scaled * gram
        paired_rows = jnp.sum(paired, axis=1, keepdims=True)
        beta_grad = jnp.sum(right_grad * rest, axis=1, keepdims=True) + paired_rows
        gram_grad = beta * scaled
        score_grad = reads_grad * part["read_decay"]
        read_pairs = reads_grad * reads
        back = mul(
            jnp.concatenate([-growth * rest_grad, part["read_growth"] * grad], axis=0), entry, tb=True
        )
        tail_grad = tail * mul(correction, leaving, tb=True)
        direct = mul(jnp.concatenate([gram_grad, score_grad], axis=0), k)
        query_grad = back[SPAN:] + direct[SPAN:]
        key_grad = (
            back[:SPAN] + direct[:SPAN] + tail_grad
            + mul(jnp.concatenate([gram_grad, score_grad], axis=0), jnp.concatenate([k, q], axis=0), ta=True)
        )
        tail_sums = jnp.sum(tail_grad * k, axis=1, keepdims=True)
        factor_cumul = (
            beta * paired_rows
            - growth * jnp.sum(rest_grad * key_entry, axis=1, keepdims=True)
            - tail_sums
        )
        token_cumul = (
            jnp.sum(read_pairs, axis=1, keepdims=True)
            + part["read_growth"] * jnp.sum(grad * query_entry, axis=1, keepdims=True)
        )
        for f in range(NF):
            token_cumul = token_cumul + factor_cumul[f * CH : (f + 1) * CH]
        last_grad = jnp.sum(tail_sums, axis=0, keepdims=True) + part["last"] * jnp.sum(
            jnp.sum(entry * leaving, axis=1, keepdims=True), axis=0, keepdims=True
        )
        token = lax.broadcasted_iota(jnp.int32, (CH, 1), 0)
        token_cumul = token_cumul + jnp.where(token == CH - 1, last_grad, 0.0)
        columns = jnp.sum(beta * paired, axis=0, keepdims=True) + jnp.sum(
            read_pairs, axis=0, keepdims=True
        )
        column_sums = columns[:, :CH]
        for f in range(1, NF):
            column_sums = column_sums + columns[:, f * CH : (f + 1) * CH]
        key_grad = part["inverse_norm"] * (
            key_grad - k * jnp.sum(k * key_grad, axis=1, keepdims=True)
        )
        dq_ref[at, :] = (query_grad * (width ** (-0.5))).astype(BF16)
        for f, (dk_ref, dv_ref) in enumerate(((dk0, dv0), (dk1, dv1), (dk2, dv2))):
            dk_ref[at, :] = key_grad[f * CH : (f + 1) * CH].astype(BF16)
            dv_ref[at, :] = rest_grad[f * CH : (f + 1) * CH].astype(BF16)
        col_out_ref[0, at, :] = jnp.concatenate(
            [beta_grad[f * CH : (f + 1) * CH] for f in range(NF)]
            + [token_cumul, jnp.zeros((CH, 4), F32)],
            axis=1,
        )
        row_out_ref[0, :, at] = jnp.broadcast_to(-column_sums, (8, CH))


def shifted(value, axis, steps):
    count = lax.axis_size(axis)
    first, last = (max(0, -steps), min(count, count - steps))
    return lax.ppermute(value, axis, [(source, source + steps) for source in range(first, last)])


def chain(total_map, total_offset, total_pull):
    turns = lax.axis_size("ctx") - 1
    high = lax.Precision.HIGHEST
    enter = jnp.zeros_like(total_offset)
    leave = jnp.zeros_like(total_pull)
    for _ in range(turns):
        enter = shifted(
            jnp.einsum("swa,sag->swg", total_map, enter, precision=high) + total_offset, "ctx", 1
        )
        leave = shifted(
            jnp.einsum("saw,sag->swg", total_map, leave, precision=high) + total_pull, "ctx", -1
        )
    return enter, leave


def on_device(
    query_input, key_input, value_input, beta_logit, gate_logit, decay_rate,
    doc_ids, out_weight, out_cotangent,
):
    high = lax.Precision.HIGHEST
    _, length, heads, width = query_input.shape
    model_width = out_cotangent.shape[-1]
    blocks = length // CH
    padded = jnp.concatenate([jnp.full((1, 1), -1, jnp.int32), doc_ids], axis=1)
    window = lax.dynamic_slice_in_dim(padded, lax.axis_index("ctx") * blocks, blocks + 1, 1)
    retain = (window[0, 1:] == window[0, :-1]).astype(F32)

    queries = query_input.reshape(length, heads * width)
    keys = key_input.reshape(length, NF * heads * width)
    values = value_input.reshape(length, NF * heads * width)
    sigmoid = jax.nn.sigmoid(beta_logit[0])
    betas = 2.0 * sigmoid
    soft = jax.nn.softplus(gate_logit[0])
    log_decay = (-decay_rate[:, None] * soft).reshape(heads, blocks, CH)
    ordered = (jnp.arange(CH)[:, None] <= jnp.arange(CH)[None, :]).astype(F32)
    cumulative = jnp.dot(log_decay, ordered, precision=high).reshape(heads, 1, length)
    rows = jnp.broadcast_to(cumulative, (heads, 8, length))
    cols = jnp.concatenate(
        [betas, cumulative, jnp.zeros((heads, 4, length), F32)], axis=1
    ).transpose(0, 2, 1)

    cot_rows = out_cotangent.reshape(length, model_width)
    core_grad = lax.dot_general(
        cot_rows, out_weight, (((1,), (1,)), ((), ())), preferred_element_type=F32
    )

    def lane_block(f):
        return pl.BlockSpec((length, width), lambda h: (0, f * heads + h))

    def whole(*shape):
        return pl.BlockSpec((1,) + shape, lambda h: (h,) + (0,) * len(shape))

    state = (width, width)
    common_specs = (
        [pl.BlockSpec(memory_space=pltpu.SMEM), lane_block(0)]
        + [lane_block(f) for f in range(NF)] * 2
        + [whole(length, 8), whole(8, length), lane_block(0)]
    )
    common = (retain, queries) + (keys,) * NF + (values,) * NF + (cols, rows, core_grad)
    saved_specs = [whole(blocks, SPAN, SPAN)] + [whole(blocks, *state)] * 3
    params = pltpu.CompilerParams(vmem_limit_bytes=48 << 20)
    per_stretch = jax.ShapeDtypeStruct((heads, blocks) + state, F32)
    per_head = jax.ShapeDtypeStruct((heads,) + state, F32)
    *saved, total_map, total_offset, total_pull = pl.pallas_call(
        functools.partial(maps_kernel, INVERSE_PASSES),
        grid=(heads,),
        in_specs=common_specs,
        out_specs=saved_specs + [whole(*state)] * 3,
        out_shape=[jax.ShapeDtypeStruct((heads, blocks, SPAN, SPAN), F32)]
        + [per_stretch] * 3
        + [per_head] * 3,
        compiler_params=params,
        name="local_maps",
    )(*common)
    enter, leave = chain(total_map, total_offset, total_pull)
    lanes = jax.ShapeDtypeStruct((length, heads * width), BF16)
    core_rows, dq, dk0, dk1, dk2, dv0, dv1, dv2, col_out, row_out = pl.pallas_call(
        functools.partial(results_kernel, RESULT_PASSES),
        grid=(heads,),
        in_specs=common_specs + saved_specs + [whole(*state)] * 2,
        out_specs=[lane_block(0)] * (2 + 2 * NF) + [whole(length, 8), whole(8, length)],
        out_shape=[lanes] * (2 + 2 * NF)
        + [
            jax.ShapeDtypeStruct((heads, length, 8), F32),
            jax.ShapeDtypeStruct((heads, 8, length), F32),
        ],
        compiler_params=params,
        name="results",
    )(*common, *saved, enter, leave)

    partial_out = jnp.dot(core_rows, out_weight, preferred_element_type=F32)
    mixed = lax.psum_scatter(partial_out, "head", scatter_dimension=1, tiled=True).astype(BF16)
    portion = lax.psum_scatter(
        jnp.einsum("td,te->de", cot_rows, core_rows, preferred_element_type=F32),
        "ctx",
        scatter_dimension=0,
        tiled=True,
    )
    weight_grad = lax.psum(portion, "dp")
    cumul_grad = (col_out[:, :, 3] + row_out[:, 0, :]).reshape(heads, blocks, CH)
    decay_grad = jnp.dot(cumul_grad, ordered.T, precision=high).reshape(heads, length)
    gate_grad = -decay_rate[:, None] * jax.nn.sigmoid(gate_logit[0]) * decay_grad
    rate_grad = lax.psum(-jnp.sum(soft * decay_grad, axis=1), ("ctx", "dp"))
    beta_grad = col_out[:, :, :NF].transpose(0, 2, 1) * (2.0 * sigmoid * (1.0 - sigmoid))

    def factors(pieces):
        return jnp.stack([p.reshape(length, heads, width) for p in pieces], axis=1)[None]

    return (
        mixed[None],
        dq.reshape(query_input.shape),
        factors((dk0, dk1, dk2)),
        factors((dv0, dv1, dv2)),
        beta_grad[None],
        gate_grad[None],
        weight_grad,
        rate_grad,
    )


INVERSE_PASSES = 3
RESULT_PASSES = 3


def solution(mesh):
    in_specs = (
        P(("groups", "dp"), "ctx", "head", None),
        P(("groups", "dp"), "ctx", None, "head", None),
        P(("groups", "dp"), "ctx", None, "head", None),
        P(("groups", "dp"), "head", None, "ctx"),
        P(("groups", "dp"), "head", "ctx"),
        P("head"),
        P(("groups", "dp"), None),
        P("head", None),
        P(("groups", "dp"), "ctx", None),
    )
    out_specs = (
        P(("groups", "dp"), "ctx", "head"),
        P(("groups", "dp"), "ctx", "head", None),
        P(("groups", "dp"), "ctx", None, "head", None),
        P(("groups", "dp"), "ctx", None, "head", None),
        P(("groups", "dp"), "head", None, "ctx"),
        P(("groups", "dp"), "head", "ctx"),
        P(("groups", "ctx"), "head"),
        P(("groups", "head")),
    )
    return jax.shard_map(
        on_device, mesh=mesh, in_specs=in_specs, out_specs=out_specs, check_vma=False
    )
```

time: 1170 us -> 365 us (0.31)
  other arithmetic: 693 us -> 7.53 us
  matrix products: 158 us -> 17.9 us
  Pallas kernels: 0 us -> 83.1 us
  local copies, waits for them, and re-layouts: 91.8 us -> 14.8 us
  waiting for transfers between devices: 144 us -> 192 us
  loops' own time: 29.3 us -> 0 us
    another operation x60 -> x0, other arithmetic: 647 us -> none  [the longest x34 641 us: stretch_step(): jax.scipy.linalg.solve_triangular(lower_factor, right_side, lower=True, u...]
    reduce_scatter x1, waiting for transfers between devices: 0.01 us -> 142 us  [on_device(): lax.psum_scatter(jnp.einsum('td,te->de', cot_rows, core_rows, preferred_e...]
    ppermute x6, waiting for transfers between devices: 144 us -> 27 us  [shifted(): lax.ppermute(value, axis, [(source, source + steps) for source in range(f...]
    dot_general x51 -> x11, matrix products: 131 us -> 17.9 us  [the longest x1 4.5 us: on_device(): jnp.einsum('td,te->de', cot_rows, core_rows, preferred_element_type=F32)]
    pallas_call x0 -> x2, Pallas kernels: none -> 83.1 us  [the longest x1 51.7 us: on_device(): pl.pallas_call(functools.partial(maps_kernel, INVERSE_PASSES), grid=(head...]
    while x344 -> x0, local copies, waits for them, and re-layouts: 47.4 us -> none
    another operation x4 -> x0, loops' own time: 29.3 us -> none  [the longest x2 29.1 us: local_pass(): closing, outputs = lax.scan(stretch_step, anchor, pieces)]
    another operation x18 -> x0, matrix products: 27 us -> none  [stretch_step(): jax.scipy.linalg.solve_triangular(lower_factor, right_side, lower=True, u...]
  transfers between devices with their start and end apart: 9 -> 9, of which waited for: 6 -> 7; matrix products, arithmetic and copies ran while one was open for 41% -> 5% of each run, Pallas kernels for 0% -> 0%
where the time goes in v1:
time: 365 us
  waiting for transfers between devices  192 us (53%)
  Pallas kernels  83.1 us (23%)
  starting transfers between devices  18.9 us (5%)
  matrix products  17.9 us (5%)
  blocking collectives  16.6 us (5%)
  local copies, waits for them, and re-layouts  14.8 us (4%)
  between operations  14.1 us (4%)
  other arithmetic  7.53 us (2%)
    reduce_scatter x1, waiting for transfers between devices, on_device(): lax.psum_scatter(jnp.einsum('td,te->de', cot_rows, core_rows, preferred_e...  142 us
    pallas_call x1, Pallas kernels, on_device(): pl.pallas_call(functools.partial(maps_kernel, INVERSE_PASSES), grid=(head...  51.7 us
    pallas_call x1, Pallas kernels, on_device(): pl.pallas_call(functools.partial(results_kernel, RESULT_PASSES), grid=(he...  31.4 us
    ppermute x6, waiting for transfers between devices, shifted(): lax.ppermute(value, axis, [(source, source + steps) for source in range(f...  27 us
    psum x1, waiting for transfers between devices, on_device(): weight_grad = lax.psum(portion, 'dp')  21.9 us
    ppermute x6, starting transfers between devices, shifted(): lax.ppermute(value, axis, [(source, source + steps) for source in range(f...  18.8 us
    psum x1, blocking collectives, on_device(): rate_grad = lax.psum(-jnp.sum(soft * decay_grad, axis=1), ('ctx', 'dp'))  16.6 us
    unnamed x37, local copies, waits for them, and re-layouts  9.79 us
  transfers between devices with their start and end apart: 9, of which 7 were waited for; matrix products, arithmetic and copies ran while one was open for 5% of the time, Pallas kernels for 0%

profile of v1, /device:TPU:0, one launch (start us, length us, event | category | flops | bytes accessed | tf_op | source)
XLA Modules:
  0.0 364.6 jit_solution(8909266195859507836)
XLA Ops:
  7.9 0.8 squeeze.6
  10.4 1.0 copy.143
  11.4 0.9 copy.96
  12.3 1.0 multiply_bitcast_fusion
  13.3 1.4 reshape.66.k0.k1.k2
  14.7 1.4 reshape.67.v0.v1.v2
  16.3 4.0 %fusion.3.grad_ref = f32[128,1024]{1,0:T(8,128)S(1)} fusion(bf16[1024,2048]{1,0:T(8,128)(2,1)} %param.16, bf16[1,128,2048]{2,1,0:T(8,128)(2,1)S(1)} %copy-done), kind=kOutput, calls=%fused_computation.14 | convolution fusion | flops 536870912 | bytes 5242880 | tf_op jit(solution)/shard_map/dot_general | solution.py:265
  20.6 51.7 %local_maps.1 = (f32[8,2,192,192]{3,2,1,0:T(8,128)}, f32[8,2,128,128]{3,2,1,0:T(8,128)S(1)}, f32[8,2,128,128]{3,2,1,0:T(8,128)}, f32[8,2,128,128]{3,2,1,0:T(8,12...) custom-call(f32[2]{0:T(128)S(1)} %fusion.15.retain_ref, ...), custom_call_target="tpu_custom_call" | custom-call | tf_op jit(solution)/shard_map/local_maps/pallas_call | solution.py:286
  72.3 1.0 convolution_add_fusion.2
  73.3 1.3 collective-permute-start.3
  75.2 5.6 %collective-permute-start = (f32[8,128,128]{2,1,0:T(8,128)S(1)}, f32[8,128,128]{2,1,0:T(8,128)S(1)}, u32[]{:S(2)}, u32[]{:S(2)}) collective-permute-start(f32[8,128,128]{2,1,0:T(8,128)S(1)} %convolution_add_fusion.5), channel_id=1, source_target_pairs={{0,4},{4,8},{8,12},{1,5},{5,9},{9,13},{2,6},{6,10},{10,14},{3,7},{... | collective-permute-start | bytes 1572872 | tf_op jit(solution)/shard_map/ppermute | solution.py:220
  80.8 9.4 %collective-permute-done.3 = f32[8,128,128]{2,1,0:T(8,128)S(1)} collective-permute-done((f32[8,128,128]{2,1,0:T(8,128)S(1)}, f32[8,128,128]{2,1,0:T(8,128)S(1)}, u32[]{:S(2)}, u32[]{:S(2)}) %collective-permute-start.3) | collective-permute-done | bytes 524320 | tf_op jit(solution)/shard_map/ppermute | solution.py:220
  90.2 1.0 convolution_add_fusion.1
  91.2 1.3 collective-permute-start.4
  93.2 4.8 %collective-permute-start.1 = (f32[8,128,128]{2,1,0:T(8,128)S(1)}, f32[8,128,128]{2,1,0:T(8,128)S(1)}, u32[]{:S(2)}, u32[]{:S(2)}) collective-permute-start(f32[8,128,128]{2,1,0:T(8,128)S(1)} %convolution_add_fusion.4), channel_id=1, source_target_pairs={{0,4},{4,8},{8,12},{1,5},{5,9},{9,13},{2,6},{6,10},{10,14},{3,7},{... | collective-permute-start | bytes 1572872 | tf_op jit(solution)/shard_map/ppermute | solution.py:220
  98.0 8.3 %collective-permute-done.4 = f32[8,128,128]{2,1,0:T(8,128)S(1)} collective-permute-done((f32[8,128,128]{2,1,0:T(8,128)S(1)}, f32[8,128,128]{2,1,0:T(8,128)S(1)}, u32[]{:S(2)}, u32[]{:S(2)}) %collective-permute-start.4) | collective-permute-done | bytes 524320 | tf_op jit(solution)/shard_map/ppermute | solution.py:220
  106.2 1.0 convolution_add_fusion
  107.3 1.3 collective-permute-start.5
  109.3 4.6 %collective-permute-start.2 = (f32[8,128,128]{2,1,0:T(8,128)S(1)}, f32[8,128,128]{2,1,0:T(8,128)S(1)}, u32[]{:S(2)}, u32[]{:S(2)}) collective-permute-start(f32[8,128,128]{2,1,0:T(8,128)S(1)} %convolution_add_fusion.3), channel_id=1, source_target_pairs={{0,4},{4,8},{8,12},{1,5},{5,9},{9,13},{2,6},{6,10},{10,14},{3,7},{... | collective-permute-start | bytes 1572872 | tf_op jit(solution)/shard_map/ppermute | solution.py:220
  113.8 7.5 %collective-permute-done.5.leave_ref = f32[8,128,128]{2,1,0:T(8,128)S(1)} collective-permute-done((f32[8,128,128]{2,1,0:T(8,128)S(1)}, f32[8,128,128]{2,1,0:T(8,128)S(1)}, u32[]{:S(2)}, u32[]{:S(2)}) %collective-permute-start.5) | collective-permute-done | bytes 524320 | tf_op jit(solution)/shard_map/ppermute | solution.py:220
  121.4 1.9 collective-permute-done.2.enter_ref
  123.2 31.4 %results.1 = (bf16[128,1024]{1,0:T(8,128)(2,1)S(1)}, bf16[128,1024]{1,0:T(8,128)(2,1)S(1)}, bf16[128,1024]{1,0:T(8,128)(2,1)S(1)}, bf16[128,1024]{1,0:T(8,128)(2...) custom-call(f32[2]{0:T(128)S(1)} %fusion.15.retain_ref, ...), custom_call_target="tpu_custom_call" | custom-call | tf_op jit(solution)/shard_map/results/pallas_call | solution.py:299
  156.7 4.5 %convolution_bitcast_fusion = f32[2048,1024]{0,1:T(8,128)} fusion(bf16[128,1024]{1,0:T(8,128)(2,1)S(1)} %get-tuple-element.32, bf16[1,128,2048]{2,1,0:T(8,128)(2,1)S(1)} %copy-done), kind=kOutput, calls=%fused_computation | convolution fusion | flops 536870912 | bytes 9175040 | tf_op jit(solution)/shard_map/td,te->de/dot_general | solution.py:316
  161.3 3.9 %fusion.19 = f32[128,2048]{1,0:T(8,128)} fusion(bf16[128,1024]{1,0:T(8,128)(2,1)S(1)} %get-tuple-element.32, bf16[1024,2048]{1,0:T(8,128)(2,1)} %param.16), kind=kOutput, calls=%fused_computation.41 | convolution fusion | flops 536870912 | bytes 5505024 | tf_op jit(solution)/shard_map/dot_general | solution.py:313
  165.3 142.2 %reduce-scatter.5.cloned.1.call-done = f32[512,1024]{0,1:T(8,128)} async-done(((f32[2048,1024]{0,1:T(8,128)}), f32[512,1024]{0,1:T(8,128)}) %reduce-scatter.5.cloned.1.call-update) | async-done | bytes 2097168 | tf_op jit(solution)/shard_map/reduce_scatter | solution.py:315
  308.4 16.6 %psum.15 = f32[8]{0:T(128)} all-reduce(f32[8]{0:T(128)S(1)} %neg.26), channel_id=1, replica_groups=mesh['groups'=2,'ctx'=4,'head'=2,'dp'=2] {'ctx','dp'}, use_global_device_ids=true, to_apply=%region_4.5 | all-reduce | flops 8 | bytes 64 | tf_op jit(solution)/shard_map/psum | solution.py:325
  325.0 0.9 fusion.1
  326.0 1.8 copy.119
  329.0 1.4 maximum_bitcast_fusion
  331.5 1.8 convert_bitcast_fusion
  333.3 21.9 %all-reduce.2.cloned.1.call-done = f32[512,1024]{0,1:T(8,128)} async-done(((f32[512,1024]{0,1:T(8,128)}), f32[512,1024]{0,1:T(8,128)}) %all-reduce.2.cloned.1.call-update) | async-done | bytes 2097168 | tf_op jit(solution)/shard_map/psum | solution.py:321
  355.2 2.9 copy.120
  (67 shorter events, 9.8 us)
Async XLA Ops:
  7.2 9.1 %copy-start = (bf16[1,128,2048]{2,1,0:T(8,128)(2,1)S(1)}, bf16[1,128,2048]{2,1,0:T(8,128)(2,1)}, u32[]{:S(2)}) copy-start(bf16[1,128,2048]{2,1,0:T(8,128)(2,1)} %param.17) | copy-start | bytes 1572868
  7.2 300.4 %reduce-scatter.5.cloned.1.call-start = ((), (), s32[]{:S(2)}) async-start(), calls=%async_computation.3 | async-start | bytes 10485760 | tf_op jit(solution)/shard_map/reduce_scatter | solution.py:315
  12.3 8.0 %copy-start.9 = (f32[1,8,3,128]{2,3,1,0:T(8,128)}, f32[1,8,3,128]{2,3,1,0:T(8,128)S(1)}, u32[]{:S(2)}) copy-start(f32[1,8,3,128]{2,3,1,0:T(8,128)S(1)} %copy.96) | copy-start | bytes 36868
  16.2 56.1 %copy-start.1 = (bf16[128,3072]{1,0:T(8,128)(2,1)}, bf16[128,3072]{1,0:T(8,128)(2,1)S(1)}, u32[]{:S(2)}) copy-start(bf16[128,3072]{1,0:T(8,128)(2,1)S(1)} %reshape.67.v0.v1.v2) | copy-start | bytes 2359300
  16.2 4.2 %copy-start.11 = (f32[8,3,128]{1,2,0:T(8,128)S(1)}, f32[8,3,128]{1,2,0:T(8,128)}, u32[]{:S(2)}) copy-start(f32[8,3,128]{1,2,0:T(8,128)} %multiply_bitcast_fusion) | copy-start | bytes 36868
  72.3 35.0 %copy-start.2 = (f32[8,2,128,128]{3,2,1,0:T(8,128)}, f32[8,2,128,128]{3,2,1,0:T(8,128)S(1)}, u32[]{:S(2)}) copy-start(f32[8,2,128,128]{3,2,1,0:T(8,128)S(1)} %get-tuple-element.26.map_ref) | copy-start | bytes 3145732
  73.3 16.9 %collective-permute-start.3 = (f32[8,128,128]{2,1,0:T(8,128)S(1)}, f32[8,128,128]{2,1,0:T(8,128)S(1)}, u32[]{:S(2)}, u32[]{:S(2)}) collective-permute-start(f32[8,128,128]{2,1,0:T(8,128)S(1)} %convolution_add_fusion.2), channel_id=1, source_target_pairs={{4,0},{8,4},{12,8},{5,1},{9,5},{13,9},{6,2},{10,6},{14,10},{7,3},{... | collective-permute-start | bytes 1572872 | tf_op jit(solution)/shard_map/ppermute | solution.py:220
  75.2 17.3 %collective-permute-start = (f32[8,128,128]{2,1,0:T(8,128)S(1)}, f32[8,128,128]{2,1,0:T(8,128)S(1)}, u32[]{:S(2)}, u32[]{:S(2)}) collective-permute-start(f32[8,128,128]{2,1,0:T(8,128)S(1)} %convolution_add_fusion.5), channel_id=1, source_target_pairs={{0,4},{4,8},{8,12},{1,5},{5,9},{9,13},{2,6},{6,10},{10,14},{3,7},{... | collective-permute-start | bytes 1572872 | tf_op jit(solution)/shard_map/ppermute | solution.py:220
  91.2 15.0 %collective-permute-start.4 = (f32[8,128,128]{2,1,0:T(8,128)S(1)}, f32[8,128,128]{2,1,0:T(8,128)S(1)}, u32[]{:S(2)}, u32[]{:S(2)}) collective-permute-start(f32[8,128,128]{2,1,0:T(8,128)S(1)} %convolution_add_fusion.1), channel_id=1, source_target_pairs={{4,0},{8,4},{12,8},{5,1},{9,5},{13,9},{6,2},{10,6},{14,10},{7,3},{... | collective-permute-start | bytes 1572872 | tf_op jit(solution)/shard_map/ppermute | solution.py:220
  93.2 15.4 %collective-permute-start.1 = (f32[8,128,128]{2,1,0:T(8,128)S(1)}, f32[8,128,128]{2,1,0:T(8,128)S(1)}, u32[]{:S(2)}, u32[]{:S(2)}) collective-permute-start(f32[8,128,128]{2,1,0:T(8,128)S(1)} %convolution_add_fusion.4), channel_id=1, source_target_pairs={{0,4},{4,8},{8,12},{1,5},{5,9},{9,13},{2,6},{6,10},{10,14},{3,7},{... | collective-permute-start | bytes 1572872 | tf_op jit(solution)/shard_map/ppermute | solution.py:220
  107.3 14.1 %collective-permute-start.5 = (f32[8,128,128]{2,1,0:T(8,128)S(1)}, f32[8,128,128]{2,1,0:T(8,128)S(1)}, u32[]{:S(2)}, u32[]{:S(2)}) collective-permute-start(f32[8,128,128]{2,1,0:T(8,128)S(1)} %convolution_add_fusion), channel_id=1, source_target_pairs={{4,0},{8,4},{12,8},{5,1},{9,5},{13,9},{6,2},{10,6},{14,10},{7,3},{... | collective-permute-start | bytes 1572872 | tf_op jit(solution)/shard_map/ppermute | solution.py:220
  109.3 14.0 %collective-permute-start.2 = (f32[8,128,128]{2,1,0:T(8,128)S(1)}, f32[8,128,128]{2,1,0:T(8,128)S(1)}, u32[]{:S(2)}, u32[]{:S(2)}) collective-permute-start(f32[8,128,128]{2,1,0:T(8,128)S(1)} %convolution_add_fusion.3), channel_id=1, source_target_pairs={{0,4},{4,8},{8,12},{1,5},{5,9},{9,13},{2,6},{6,10},{10,14},{3,7},{... | collective-permute-start | bytes 1572872 | tf_op jit(solution)/shard_map/ppermute | solution.py:220
  154.6 0.7 copy-start.3
  155.3 0.7 copy-start.5
  156.0 0.7 copy-start.7
  161.3 163.7 %copy-start.10 = (f32[1,8,3,128]{2,3,1,0:T(8,128)S(1)}, f32[1,8,3,128]{2,3,1,0:T(8,128)}, u32[]{:S(2)}) copy-start(f32[1,8,3,128]{2,3,1,0:T(8,128)} %copy-done.9) | copy-start | bytes 36868
  161.3 170.2 %reduce-scatter.3.cloned.1.call-start = ((), (), s32[]{:S(2)}) async-start(), calls=%async_computation.2 | async-start | bytes 1572864 | tf_op jit(solution)/shard_map/reduce_scatter | solution.py:314
  165.3 162.5 %copy-start.8 = (bf16[128,1024]{1,0:T(8,128)(2,1)S(1)}, bf16[128,1024]{1,0:T(8,128)(2,1)}, u32[]{:S(2)}) copy-start(bf16[128,1024]{1,0:T(8,128)(2,1)} %copy-done.7) | copy-start | bytes 786436
  165.3 163.3 %copy-start.6 = (bf16[128,1024]{1,0:T(8,128)(2,1)S(1)}, bf16[128,1024]{1,0:T(8,128)(2,1)}, u32[]{:S(2)}) copy-start(bf16[128,1024]{1,0:T(8,128)(2,1)} %copy-done.5) | copy-start | bytes 786436
  165.3 163.4 %copy-start.4 = (bf16[128,1024]{1,0:T(8,128)(2,1)S(1)}, bf16[128,1024]{1,0:T(8,128)(2,1)}, u32[]{:S(2)}) copy-start(bf16[128,1024]{1,0:T(8,128)(2,1)} %copy-done.3) | copy-start | bytes 786436
  165.3 189.9 %all-reduce.2.cloned.1.call-start = ((), (), s32[]{:S(2)}) async-start(), calls=%async_computation.4 | async-start | bytes 4194304 | tf_op jit(solution)/shard_map/psum | solution.py:321
  325.0 5.4 %copy-start.12 = (f32[1,8,128]{2,1,0:T(8,128)S(1)}, f32[1,8,128]{2,1,0:T(8,128)}, u32[]{:S(2)}) copy-start(f32[1,8,128]{2,1,0:T(8,128)} %param.13) | copy-start | bytes 12292
Sparse Core Ops, SparseCore 0:
  161.4 146.1 reduce-scatter.4
  310.4 21.0 reduce-scatter.2
  333.9 21.2 all-reduce.1

commit v2 on v1

--- a/solution.py
+++ b/solution.py
@@ -214,10 +214,43 @@
         row_out_ref[0, :, at] = jnp.broadcast_to(-column_sums, (8, CH))
 
 
+def widen_kernel(narrow_ref, wide_ref):
+    wide_ref[...] = narrow_ref[...].astype(F32)
+
+
 def shifted(value, axis, steps):
     count = lax.axis_size(axis)
     first, last = (max(0, -steps), min(count, count - steps))
     return lax.ppermute(value, axis, [(source, source + steps) for source in range(first, last)])
+
+
+def cyclic(value, axis, steps):
+    count = lax.axis_size(axis)
+    if steps == 0:
+        return value
+    moved = lax.ppermute(
+        lax.optimization_barrier(value), axis, [(i, (i + steps) % count) for i in range(count)]
+    )
+    return lax.optimization_barrier(moved)
+
+
+def column_slab(value, step, axis):
+    count = lax.axis_size(axis)
+    size = value.shape[1] // count
+    owner = lax.rem(lax.axis_index(axis) + step, count)
+    return lax.dynamic_slice_in_dim(value, owner * size, size, 1)
+
+
+def scattered_sum(value, axis):
+    return sum(
+        cyclic(column_slab(value, step, axis), axis, step) for step in range(lax.axis_size(axis))
+    )
+
+
+def exchanged_sum(value, axis):
+    if lax.axis_size(axis) == 2:
+        return value + cyclic(value, axis, 1)
+    return lax.psum(value, axis)
 
 
 def chain(total_map, total_offset, total_pull):
@@ -262,6 +295,14 @@
     ).transpose(0, 2, 1)
 
     cot_rows = out_cotangent.reshape(length, model_width)
+    ctx_size = lax.axis_size("ctx")
+    slab_width = model_width // ctx_size
+    wide_rows = pl.pallas_call(
+        widen_kernel, out_shape=jax.ShapeDtypeStruct(cot_rows.shape, F32), name="widen"
+    )(cot_rows)
+    slabs = [
+        cyclic(column_slab(wide_rows, step, "ctx"), "ctx", step) for step in range(ctx_size)
+    ]
     core_grad = lax.dot_general(
         cot_rows, out_weight, (((1,), (1,)), ((), ())), preferred_element_type=F32
     )
@@ -310,19 +351,32 @@
         name="results",
     )(*common, *saved, enter, leave)
 
-    partial_out = jnp.dot(core_rows, out_weight, preferred_element_type=F32)
-    mixed = lax.psum_scatter(partial_out, "head", scatter_dimension=1, tiled=True).astype(BF16)
-    portion = lax.psum_scatter(
-        jnp.einsum("td,te->de", cot_rows, core_rows, preferred_element_type=F32),
-        "ctx",
-        scatter_dimension=0,
-        tiled=True,
-    )
-    weight_grad = lax.psum(portion, "dp")
     cumul_grad = (col_out[:, :, 3] + row_out[:, 0, :]).reshape(heads, blocks, CH)
     decay_grad = jnp.dot(cumul_grad, ordered.T, precision=high).reshape(heads, length)
     gate_grad = -decay_rate[:, None] * jax.nn.sigmoid(gate_logit[0]) * decay_grad
-    rate_grad = lax.psum(-jnp.sum(soft * decay_grad, axis=1), ("ctx", "dp"))
+    rate_part = jnp.pad(-jnp.sum(soft * decay_grad, axis=1), (0, (width - 1) * heads))
+    sent = jnp.concatenate(
+        [core_rows.astype(F32), jnp.broadcast_to(rate_part, (8, heads * width))], axis=0
+    )
+    gathered = lax.optimization_barrier(lax.all_gather(sent, "ctx", axis=0))
+    sources = [lax.rem(lax.axis_index("ctx") - step + ctx_size, ctx_size) for step in range(ctx_size)]
+    partial_weight = sum(
+        lax.dot_general(
+            slab,
+            lax.dynamic_index_in_dim(gathered, source, 0, keepdims=False)[:length],
+            (((0,), (0,)), ((), ())),
+            precision=high,
+            preferred_element_type=F32,
+        )
+        for slab, source in zip(slabs, sources)
+    )
+    totals = exchanged_sum(
+        jnp.concatenate([partial_weight, jnp.sum(gathered[:, length:], axis=0)], axis=0), "dp"
+    )
+    weight_grad = totals[:slab_width]
+    rate_grad = totals[slab_width, :heads]
+    partial_out = jnp.dot(core_rows, out_weight, preferred_element_type=F32)
+    mixed = scattered_sum(partial_out, "head").astype(BF16)
     beta_grad = col_out[:, :, :NF].transpose(0, 2, 1) * (2.0 * sigmoid * (1.0 - sigmoid))
 
     def factors(pieces):

time: 365 us -> 267 us (0.73)
  waiting for transfers between devices: 192 us -> 89.7 us
  blocking collectives: 16.6 us -> 0 us
  starting transfers between devices: 18.9 us -> 26.4 us
  other arithmetic: 7.53 us -> 12.5 us
  matrix products: 17.9 us -> 21.9 us
    reduce_scatter x2 -> x0, waiting for transfers between devices: 143 us -> none  [the longest x1 142 us: on_device(): lax.psum_scatter(jnp.einsum('td,te->de', cot_rows, core_rows, preferred_e...]
    ppermute x0 -> x5, waiting for transfers between devices: none -> 33.6 us  [cyclic(): lax.ppermute(lax.optimization_barrier(value), axis, [(i, (i + steps) % co...]
    all_gather x0 -> x1, waiting for transfers between devices: none -> 29.1 us  [on_device(): gathered = lax.optimization_barrier(lax.all_gather(sent, 'ctx', axis=0))]
    psum x1 -> x0, waiting for transfers between devices: 21.9 us -> none  [on_device(): weight_grad = lax.psum(portion, 'dp')]
    psum x1 -> x0, blocking collectives: 16.6 us -> none  [on_device(): rate_grad = lax.psum(-jnp.sum(soft * decay_grad, axis=1), ('ctx', 'dp'))]
    ppermute x0 -> x5, starting transfers between devices: none -> 7.55 us  [cyclic(): lax.ppermute(lax.optimization_barrier(value), axis, [(i, (i + steps) % co...]
    dot_general x1 -> x4, matrix products: 4.5 us -> 9.72 us  [on_device(): lax.dot_general(slab, lax.dynamic_index_in_dim(gathered, source, 0, keepd...]
    unnamed x37 -> x34, local copies, waits for them, and re-layouts: 9.79 us -> 7.04 us
  transfers between devices with their start and end apart: 9 -> 12, of which waited for: 7 -> 9; matrix products, arithmetic and copies ran while one was open for 5% -> 7% of each run, Pallas kernels for 0% -> 1%
where the time goes in v2:
time: 267 us; the launch traced here: 266 us
  waiting for transfers between devices  89.7 us (34%)
  Pallas kernels  85.2 us (32%)
  starting transfers between devices  26.4 us (10%)
  matrix products  21.9 us (8%)
  local copies, waits for them, and re-layouts  15.8 us (6%)
  between operations  14.5 us (5%)
  other arithmetic  12.5 us (5%)
    pallas_call x1, Pallas kernels, on_device(): pl.pallas_call(functools.partial(maps_kernel, INVERSE_PASSES), grid=(head...  51.7 us
    ppermute x5, waiting for transfers between devices, cyclic(): lax.ppermute(lax.optimization_barrier(value), axis, [(i, (i + steps) % co...  33.6 us
    pallas_call x1, Pallas kernels, on_device(): pl.pallas_call(functools.partial(results_kernel, RESULT_PASSES), grid=(he...  31.4 us
    all_gather x1, waiting for transfers between devices, on_device(): gathered = lax.optimization_barrier(lax.all_gather(sent, 'ctx', axis=0))  29.1 us
    ppermute x6, waiting for transfers between devices, shifted(): lax.ppermute(value, axis, [(source, source + steps) for source in range(f...  27 us
    ppermute x6, starting transfers between devices, shifted(): lax.ppermute(value, axis, [(source, source + steps) for source in range(f...  18.8 us
    dot_general x4, matrix products, on_device(): lax.dot_general(slab, lax.dynamic_index_in_dim(gathered, source, 0, keepd...  9.72 us
    ppermute x5, starting transfers between devices, cyclic(): lax.ppermute(lax.optimization_barrier(value), axis, [(i, (i + steps) % co...  7.55 us
  transfers between devices with their start and end apart: 12, of which 9 were waited for; matrix products, arithmetic and copies ran while one was open for 7% of the time, Pallas kernels for 1%

profile of v2, /device:TPU:0, one launch (start us, length us, event | category | flops | bytes accessed | tf_op | source)
XLA Modules:
  0.0 266.1 jit_solution(341477129631404431)
XLA Ops:
  12.6 1.4 reshape.71.v0.v1.v2
  14.2 3.8 %fusion.23.grad_ref = f32[128,1024]{1,0:T(8,128)S(1)} fusion(bf16[1024,2048]{1,0:T(8,128)(2,1)} %param.16, bf16[1,128,2048]{2,1,0:T(8,128)(2,1)S(1)} %copy-done.7), kind=kOutput, calls=%fused_computation.57 | convolution fusion | flops 536870912 | bytes 5242880 | tf_op jit(solution)/shard_map/dot_general | solution.py:306
  18.3 51.7 %local_maps.1 = (f32[8,2,192,192]{3,2,1,0:T(8,128)}, f32[8,2,128,128]{3,2,1,0:T(8,128)S(1)}, f32[8,2,128,128]{3,2,1,0:T(8,128)}, f32[8,2,128,128]{3,2,1,0:T(8,12...) custom-call(f32[2]{0:T(128)S(1)} %fusion.22.retain_ref, ...), custom_call_target="tpu_custom_call" | custom-call | tf_op jit(solution)/shard_map/local_maps/pallas_call | solution.py:327
  72.9 5.6 %collective-permute-start = (f32[8,128,128]{2,1,0:T(8,128)S(1)}, f32[8,128,128]{2,1,0:T(8,128)S(1)}, u32[]{:S(2)}, u32[]{:S(2)}) collective-permute-start(f32[8,128,128]{2,1,0:T(8,128)S(1)} %convolution_add_fusion.5), channel_id=1, source_target_pairs={{0,4},{4,8},{8,12},{1,5},{5,9},{9,13},{2,6},{6,10},{10,14},{3,7},{... | collective-permute-start | bytes 1572872 | tf_op jit(solution)/shard_map/ppermute | solution.py:224
  78.5 9.4 %collective-permute-done.3 = f32[8,128,128]{2,1,0:T(8,128)S(1)} collective-permute-done((f32[8,128,128]{2,1,0:T(8,128)S(1)}, f32[8,128,128]{2,1,0:T(8,128)S(1)}, u32[]{:S(2)}, u32[]{:S(2)}) %collective-permute-start.3) | collective-permute-done | bytes 524320 | tf_op jit(solution)/shard_map/ppermute | solution.py:224
  90.9 4.8 %collective-permute-start.1 = (f32[8,128,128]{2,1,0:T(8,128)S(1)}, f32[8,128,128]{2,1,0:T(8,128)S(1)}, u32[]{:S(2)}, u32[]{:S(2)}) collective-permute-start(f32[8,128,128]{2,1,0:T(8,128)S(1)} %convolution_add_fusion.4), channel_id=1, source_target_pairs={{0,4},{4,8},{8,12},{1,5},{5,9},{9,13},{2,6},{6,10},{10,14},{3,7},{... | collective-permute-start | bytes 1572872 | tf_op jit(solution)/shard_map/ppermute | solution.py:224
  95.7 8.3 %collective-permute-done.4 = f32[8,128,128]{2,1,0:T(8,128)S(1)} collective-permute-done((f32[8,128,128]{2,1,0:T(8,128)S(1)}, f32[8,128,128]{2,1,0:T(8,128)S(1)}, u32[]{:S(2)}, u32[]{:S(2)}) %collective-permute-start.4) | collective-permute-done | bytes 524320 | tf_op jit(solution)/shard_map/ppermute | solution.py:224
  107.0 4.6 %collective-permute-start.2 = (f32[8,128,128]{2,1,0:T(8,128)S(1)}, f32[8,128,128]{2,1,0:T(8,128)S(1)}, u32[]{:S(2)}, u32[]{:S(2)}) collective-permute-start(f32[8,128,128]{2,1,0:T(8,128)S(1)} %convolution_add_fusion.3), channel_id=1, source_target_pairs={{0,4},{4,8},{8,12},{1,5},{5,9},{9,13},{2,6},{6,10},{10,14},{3,7},{... | collective-permute-start | bytes 1572872 | tf_op jit(solution)/shard_map/ppermute | solution.py:224
  111.6 7.5 %collective-permute-done.5.leave_ref = f32[8,128,128]{2,1,0:T(8,128)S(1)} collective-permute-done((f32[8,128,128]{2,1,0:T(8,128)S(1)}, f32[8,128,128]{2,1,0:T(8,128)S(1)}, u32[]{:S(2)}, u32[]{:S(2)}) %collective-permute-start.5) | collective-permute-done | bytes 524320 | tf_op jit(solution)/shard_map/ppermute | solution.py:224
  119.1 1.9 collective-permute-done.2.enter_ref
  121.0 31.4 %results.1 = (bf16[128,1024]{1,0:T(8,128)(2,1)S(1)}, bf16[128,1024]{1,0:T(8,128)(2,1)S(1)}, bf16[128,1024]{1,0:T(8,128)(2,1)S(1)}, bf16[128,1024]{1,0:T(8,128)(2...) custom-call(f32[2]{0:T(128)S(1)} %fusion.22.retain_ref, ...), custom_call_target="tpu_custom_call" | custom-call | tf_op jit(solution)/shard_map/results/pallas_call | solution.py:340
  154.2 2.1 widen.1
  156.3 2.0 constant_dynamic-slice_fusion
  158.3 2.5 collective-permute-start.7
  160.7 2.1 collective-permute-start.8
  162.8 1.4 collective-permute-start.9
  164.2 6.9 %collective-permute-done.7 = f32[128,512]{1,0:T(8,128)S(1)} collective-permute-done((f32[128,512]{1,0:T(8,128)}, f32[128,512]{1,0:T(8,128)S(1)}, u32[]{:S(2)}, u32[]{:S(2)}) %collective-permute-start.7) | collective-permute-done | bytes 262176 | tf_op jit(solution)/shard_map/ppermute | solution.py:231
  171.1 17.6 %collective-permute-done.8 = f32[128,512]{1,0:T(8,128)S(1)} collective-permute-done((f32[128,512]{1,0:T(8,128)}, f32[128,512]{1,0:T(8,128)S(1)}, u32[]{:S(2)}, u32[]{:S(2)}) %collective-permute-start.8) | collective-permute-done | bytes 262176 | tf_op jit(solution)/shard_map/ppermute | solution.py:231
  189.8 29.1 %all-gather.3.cloned.1.call-done = f32[544,1024]{1,0:T(8,128)} async-done(((f32[136,1024]{1,0:T(8,128)}), f32[544,1024]{1,0:T(8,128)}) %all-gather.3.cloned.1.call-update) | async-done | bytes 2228240 | tf_op jit(solution)/shard_map/all_gather | solution.py:361
  219.9 2.9 %fusion.2 = f32[512,1024]{1,0:T(8,128)S(1)} fusion(f32[128,512]{1,0:T(8,128)S(1)} %collective-permute-done.7, f32[4,136,1024]{2,1,0:T(8,128)} %bitcast.124, s32[]{:T(128)S(6)} %select_n.47), kind=kOutput, calls=%fused_computation.16 | convolution fusion | flops 805306368 | bytes 2883588 | tf_op jit(solution)/shard_map/dot_general | solution.py:364
  222.8 1.8 fusion.1
  224.7 2.8 %fusion.3 = f32[512,1024]{1,0:T(8,128)S(1)} fusion(f32[4,136,1024]{2,1,0:T(8,128)S(1)} %bitcast.126, s32[]{:T(128)S(6)} %select_n.45, f32[128,2048]{1,0:T(8,128)} %widen.1, s32[]{:T(128)S(6)} %select_n.44), kind=kOutput, calls=%fused_computation.18 | convolution fusion | flops 805306368 | bytes 2883592 | tf_op jit(solution)/shard_map/dot_general | solution.py:364
  227.5 2.2 add_add_fusion
  229.7 1.3 copy-done.2
  231.0 1.5 pad_maximum_fusion
  235.0 3.0 %fusion.29 = f32[128,2048]{1,0:T(8,128)S(1)} fusion(bf16[128,1024]{1,0:T(8,128)(2,1)S(1)} %get-tuple-element.32, bf16[1024,2048]{1,0:T(8,128)(2,1)} %param.16), kind=kOutput, calls=%fused_computation.63 | convolution fusion | flops 536870912 | bytes 5505024 | tf_op jit(solution)/shard_map/dot_general | solution.py:378
  238.9 1.6 collective-permute-start.6
  242.1 2.6 maximum_bitcast_fusion
  245.4 8.0 %collective-permute-done.6 = f32[128,1024]{1,0:T(8,128)} collective-permute-done((f32[128,1024]{1,0:T(8,128)}, f32[128,1024]{1,0:T(8,128)}, u32[]{:S(2)}, u32[]{:S(2)}) %collective-permute-start.6) | collective-permute-done | bytes 524320 | tf_op jit(solution)/shard_map/ppermute | solution.py:231
  253.5 1.8 fusion.6
  255.3 2.0 fusion.28
  257.3 1.5 slice.65
  (82 shorter events, 24.7 us)
Async XLA Ops:
  7.2 5.1 %copy-start.9 = (bf16[1,128,3,8,128]{4,3,2,1,0:T(8,128)(2,1)S(1)}, bf16[1,128,3,8,128]{4,3,2,1,0:T(8,128)(2,1)}, u32[]{:S(2)}) copy-start(bf16[1,128,3,8,128]{4,3,2,1,0:T(8,128)(2,1)} %param.10) | copy-start | bytes 2359300
  7.2 211.7 %all-gather.3.cloned.1.call-start = ((), (), s32[]{:S(2)}) async-start(), calls=%async_computation | async-start | bytes 2785280 | tf_op jit(solution)/shard_map/all_gather | solution.py:361
  11.3 0.8 copy-start.4
  12.1 2.0 copy-start.10
  12.1 2.1 copy-start.7
  14.1 4.2 %copy-start = (bf16[128,3072]{1,0:T(8,128)(2,1)}, bf16[128,3072]{1,0:T(8,128)(2,1)S(1)}, u32[]{:S(2)}) copy-start(bf16[128,3072]{1,0:T(8,128)(2,1)S(1)} %reshape.71.v0.v1.v2) | copy-start | bytes 2359300
  70.0 18.9 %copy-start.1 = (f32[8,2,128,128]{3,2,1,0:T(8,128)}, f32[8,2,128,128]{3,2,1,0:T(8,128)S(1)}, u32[]{:S(2)}) copy-start(f32[8,2,128,128]{3,2,1,0:T(8,128)S(1)} %get-tuple-element.26.map_ref) | copy-start | bytes 3145732
  71.0 16.9 %collective-permute-start.3 = (f32[8,128,128]{2,1,0:T(8,128)S(1)}, f32[8,128,128]{2,1,0:T(8,128)S(1)}, u32[]{:S(2)}, u32[]{:S(2)}) collective-permute-start(f32[8,128,128]{2,1,0:T(8,128)S(1)} %convolution_add_fusion.2), channel_id=1, source_target_pairs={{4,0},{8,4},{12,8},{5,1},{9,5},{13,9},{6,2},{10,6},{14,10},{7,3},{... | collective-permute-start | bytes 1572872 | tf_op jit(solution)/shard_map/ppermute | solution.py:224
  72.9 17.4 %collective-permute-start = (f32[8,128,128]{2,1,0:T(8,128)S(1)}, f32[8,128,128]{2,1,0:T(8,128)S(1)}, u32[]{:S(2)}, u32[]{:S(2)}) collective-permute-start(f32[8,128,128]{2,1,0:T(8,128)S(1)} %convolution_add_fusion.5), channel_id=1, source_target_pairs={{0,4},{4,8},{8,12},{1,5},{5,9},{9,13},{2,6},{6,10},{10,14},{3,7},{... | collective-permute-start | bytes 1572872 | tf_op jit(solution)/shard_map/ppermute | solution.py:224
  89.0 15.0 %collective-permute-start.4 = (f32[8,128,128]{2,1,0:T(8,128)S(1)}, f32[8,128,128]{2,1,0:T(8,128)S(1)}, u32[]{:S(2)}, u32[]{:S(2)}) collective-permute-start(f32[8,128,128]{2,1,0:T(8,128)S(1)} %convolution_add_fusion.1), channel_id=1, source_target_pairs={{4,0},{8,4},{12,8},{5,1},{9,5},{13,9},{6,2},{10,6},{14,10},{7,3},{... | collective-permute-start | bytes 1572872 | tf_op jit(solution)/shard_map/ppermute | solution.py:224
  90.9 15.4 %collective-permute-start.1 = (f32[8,128,128]{2,1,0:T(8,128)S(1)}, f32[8,128,128]{2,1,0:T(8,128)S(1)}, u32[]{:S(2)}, u32[]{:S(2)}) collective-permute-start(f32[8,128,128]{2,1,0:T(8,128)S(1)} %convolution_add_fusion.4), channel_id=1, source_target_pairs={{0,4},{4,8},{8,12},{1,5},{5,9},{9,13},{2,6},{6,10},{10,14},{3,7},{... | collective-permute-start | bytes 1572872 | tf_op jit(solution)/shard_map/ppermute | solution.py:224
  105.0 14.1 %collective-permute-start.5 = (f32[8,128,128]{2,1,0:T(8,128)S(1)}, f32[8,128,128]{2,1,0:T(8,128)S(1)}, u32[]{:S(2)}, u32[]{:S(2)}) collective-permute-start(f32[8,128,128]{2,1,0:T(8,128)S(1)} %convolution_add_fusion), channel_id=1, source_target_pairs={{4,0},{8,4},{12,8},{5,1},{9,5},{13,9},{6,2},{10,6},{14,10},{7,3},{... | collective-permute-start | bytes 1572872 | tf_op jit(solution)/shard_map/ppermute | solution.py:224
  107.0 14.0 %collective-permute-start.2 = (f32[8,128,128]{2,1,0:T(8,128)S(1)}, f32[8,128,128]{2,1,0:T(8,128)S(1)}, u32[]{:S(2)}, u32[]{:S(2)}) collective-permute-start(f32[8,128,128]{2,1,0:T(8,128)S(1)} %convolution_add_fusion.3), channel_id=1, source_target_pairs={{0,4},{4,8},{8,12},{1,5},{5,9},{9,13},{2,6},{6,10},{10,14},{3,7},{... | collective-permute-start | bytes 1572872 | tf_op jit(solution)/shard_map/ppermute | solution.py:224
  158.3 12.9 %collective-permute-start.7 = (f32[128,512]{1,0:T(8,128)}, f32[128,512]{1,0:T(8,128)S(1)}, u32[]{:S(2)}, u32[]{:S(2)}) collective-permute-start(f32[128,512]{1,0:T(8,128)} %get-tuple-element.84), channel_id=1, source_target_pairs={{0,4},{4,8},{8,12},{12,0},{1,5},{5,9},{9,13},{13,1},{2,6},{6,10},{... | collective-permute-start | bytes 786440 | tf_op jit(solution)/shard_map/ppermute | solution.py:231
  160.7 28.0 %collective-permute-start.8 = (f32[128,512]{1,0:T(8,128)}, f32[128,512]{1,0:T(8,128)S(1)}, u32[]{:S(2)}, u32[]{:S(2)}) collective-permute-start(f32[128,512]{1,0:T(8,128)} %get-tuple-element.83), channel_id=1, source_target_pairs={{0,8},{4,12},{8,0},{12,4},{1,9},{5,13},{9,1},{13,5},{2,10},{6,14},... | collective-permute-start | bytes 786440 | tf_op jit(solution)/shard_map/ppermute | solution.py:231
  162.8 26.9 %collective-permute-start.9 = (f32[128,512]{1,0:T(8,128)}, f32[128,512]{1,0:T(8,128)S(1)}, u32[]{:S(2)}, u32[]{:S(2)}) collective-permute-start(f32[128,512]{1,0:T(8,128)} %get-tuple-element.82), channel_id=1, source_target_pairs={{0,12},{4,0},{8,4},{12,8},{1,13},{5,1},{9,5},{13,9},{2,14},{6,2},{... | collective-permute-start | bytes 786440 | tf_op jit(solution)/shard_map/ppermute | solution.py:231
  218.9 4.0 %copy-start.6 = (f32[544,1024]{1,0:T(8,128)S(1)}, f32[544,1024]{1,0:T(8,128)}, u32[]{:S(2)}) copy-start(f32[544,1024]{1,0:T(8,128)} %all-gather.3.cloned.1.call-done) | copy-start | bytes 6684676
  229.7 1.3 copy-start.2
  232.5 22.8 %collective-permute-start.10 = (f32[520,1024]{1,0:T(8,128)}, f32[520,1024]{1,0:T(8,128)}, u32[]{:S(2)}, u32[]{:S(2)}) collective-permute-start(f32[520,1024]{1,0:T(8,128)} %pad_maximum_fusion), channel_id=1, source_target_pairs={{0,1},{1,0},{2,3},{3,2},{4,5},{5,4},{6,7},{7,6},{8,9},{9,8},{10,11... | collective-permute-start | bytes 6389768 | tf_op jit(solution)/shard_map/ppermute | solution.py:231
  235.0 5.4 %copy-start.5 = (f32[1,8,3,128]{2,3,1,0:T(8,128)S(1)}, f32[1,8,3,128]{2,3,1,0:T(8,128)}, u32[]{:S(2)}) copy-start(f32[1,8,3,128]{2,3,1,0:T(8,128)} %copy-done.4) | copy-start | bytes 36868
  238.0 4.1 %copy-start.8 = (bf16[16,8,8,128]{3,2,1,0:T(8,128)(2,1)S(1)}, bf16[16,8,8,128]{3,2,1,0:T(8,128)(2,1)}, u32[]{:S(2)}) copy-start(bf16[16,8,8,128]{3,2,1,0:T(8,128)(2,1)} %copy.121) | copy-start | bytes 786436
  238.9 14.6 %collective-permute-start.6 = (f32[128,1024]{1,0:T(8,128)}, f32[128,1024]{1,0:T(8,128)}, u32[]{:S(2)}, u32[]{:S(2)}) collective-permute-start(f32[128,1024]{1,0:T(8,128)} %constant_dynamic-slice_fusion.3), channel_id=1, source_target_pairs={{0,2},{2,0},{1,3},{3,1},{4,6},{6,4},{5,7},{7,5},{8,10},{10,8},{9,1... | collective-permute-start | bytes 1572872 | tf_op jit(solution)/shard_map/ppermute | solution.py:231
  240.6 4.2 %copy-start.11 = (f32[1,8,128]{2,1,0:T(8,128)S(1)}, f32[1,8,128]{2,1,0:T(8,128)}, u32[]{:S(2)}) copy-start(f32[1,8,128]{2,1,0:T(8,128)} %param.13) | copy-start | bytes 12292
  242.1 13.1 %copy-start.3 = (f32[512,1024]{1,0:T(8,128)S(1)}, f32[512,1024]{1,0:T(8,128)}, u32[]{:S(2)}) copy-start(f32[512,1024]{1,0:T(8,128)} %copy-done.2) | copy-start | bytes 6291460
Sparse Core Ops, SparseCore 0:
  154.3 64.5 all-gather.2

commit v3 on v2

--- a/solution.py
+++ b/solution.py
@@ -333,8 +333,12 @@
         + [per_stretch] * 3
         + [per_head] * 3,
         compiler_params=params,
+        cost_estimate=pl.CostEstimate(
+            flops=6000 * heads * blocks * SPAN**3 // 64, bytes_accessed=16 << 20, transcendentals=0
+        ),
         name="local_maps",
     )(*common)
+    total_map, slabs = lax.optimization_barrier((total_map, slabs))
     enter, leave = chain(total_map, total_offset, total_pull)
     lanes = jax.ShapeDtypeStruct((length, heads * width), BF16)
     core_rows, dq, dk0, dk1, dk2, dv0, dv1, dv2, col_out, row_out = pl.pallas_call(

time: 267 us -> 256 us (0.959)
  waiting for transfers between devices: 89.7 us -> 80.4 us
    ppermute x5, waiting for transfers between devices: 33.6 us -> 8.2 us  [cyclic(): lax.ppermute(lax.optimization_barrier(value), axis, [(i, (i + steps) % co...]
    all_gather x1, waiting for transfers between devices: 29.1 us -> 48.7 us  [on_device(): gathered = lax.optimization_barrier(lax.all_gather(sent, 'ctx', axis=0))]
    ppermute x6, waiting for transfers between devices: 27 us -> 23.5 us  [shifted(): lax.ppermute(value, axis, [(source, source + steps) for source in range(f...]
    unnamed x34 -> x44, local copies, waits for them, and re-layouts: 7.04 us -> 6.23 us
  transfers between devices with their start and end apart: 12 -> 12, of which waited for: 9 -> 6; matrix products, arithmetic and copies ran while one was open for 7% -> 10% of each run, Pallas kernels for 1% -> 20%
where the time goes in v3:
time: 256 us; the launch traced here: 255 us
  Pallas kernels  85.2 us (33%)
  waiting for transfers between devices  80.4 us (31%)
  starting transfers between devices  26.3 us (10%)
  matrix products  22.1 us (9%)
  local copies, waits for them, and re-layouts  15.6 us (6%)
  between operations  14.6 us (6%)
  other arithmetic  11.2 us (4%)
    pallas_call x1, Pallas kernels, on_device(): pl.pallas_call(functools.partial(maps_kernel, INVERSE_PASSES), grid=(head...  51.8 us
    all_gather x1, waiting for transfers between devices, on_device(): gathered = lax.optimization_barrier(lax.all_gather(sent, 'ctx', axis=0))  48.7 us
    pallas_call x1, Pallas kernels, on_device(): pl.pallas_call(functools.partial(results_kernel, RESULT_PASSES), grid=(he...  31.4 us
    ppermute x6, waiting for transfers between devices, shifted(): lax.ppermute(value, axis, [(source, source + steps) for source in range(f...  23.5 us
    ppermute x6, starting transfers between devices, shifted(): lax.ppermute(value, axis, [(source, source + steps) for source in range(f...  17.8 us
    dot_general x4, matrix products, on_device(): lax.dot_general(slab, lax.dynamic_index_in_dim(gathered, source, 0, keepd...  9.79 us
    ppermute x5, starting transfers between devices, cyclic(): lax.ppermute(lax.optimization_barrier(value), axis, [(i, (i + steps) % co...  8.43 us
    ppermute x5, waiting for transfers between devices, cyclic(): lax.ppermute(lax.optimization_barrier(value), axis, [(i, (i + steps) % co...  8.2 us
  transfers between devices with their start and end apart: 12, of which 6 were waited for; matrix products, arithmetic and copies ran while one was open for 10% of the time, Pallas kernels for 20%

profile of v3, /device:TPU:0, one launch (start us, length us, event | category | flops | bytes accessed | tf_op | source)
XLA Modules:
  0.0 255.3 jit_solution(1079605243082501762)
XLA Ops:
  7.3 2.1 widen.1
  9.4 2.2 constant_dynamic-slice_fusion.1
  11.5 3.0 %collective-permute-start = (f32[128,512]{1,0:T(8,128)}, f32[128,512]{1,0:T(8,128)}, u32[]{:S(2)}, u32[]{:S(2)}) collective-permute-start(f32[128,512]{1,0:T(8,128)} %get-tuple-element.94), channel_id=1, source_target_pairs={{0,4},{4,8},{8,12},{12,0},{1,5},{5,9},{9,13},{13,1},{2,6},{6,10},{... | collective-permute-start | bytes 786440 | tf_op jit(solution)/shard_map/ppermute | solution.py:231
  14.6 2.6 %collective-permute-start.1 = (f32[128,512]{1,0:T(8,128)}, f32[128,512]{1,0:T(8,128)S(1)}, u32[]{:S(2)}, u32[]{:S(2)}) collective-permute-start(f32[128,512]{1,0:T(8,128)} %get-tuple-element.93), channel_id=1, source_target_pairs={{0,8},{4,12},{8,0},{12,4},{1,9},{5,13},{9,1},{13,5},{2,10},{6,14},... | collective-permute-start | bytes 786440 | tf_op jit(solution)/shard_map/ppermute | solution.py:231
  17.2 1.3 collective-permute-start.2
  20.6 1.4 reshape.70.k0.k1.k2
  22.1 1.4 reshape.71.v0.v1.v2
  23.6 4.0 %fusion.21.grad_ref = f32[128,1024]{1,0:T(8,128)S(1)} fusion(bf16[1024,2048]{1,0:T(8,128)(2,1)} %param.16, bf16[1,128,2048]{2,1,0:T(8,128)(2,1)S(1)} %copy-done.7), kind=kOutput, calls=%fused_computation.56 | convolution fusion | flops 536870912 | bytes 5242880 | tf_op jit(solution)/shard_map/dot_general | solution.py:306
  27.9 51.8 %local_maps.1 = (f32[8,2,192,192]{3,2,1,0:T(8,128)}, f32[8,2,128,128]{3,2,1,0:T(8,128)S(1)}, f32[8,2,128,128]{3,2,1,0:T(8,128)}, f32[8,2,128,128]{3,2,1,0:T(8,12...) custom-call(f32[2]{0:T(128)S(1)} %fusion.20.retain_ref, ...), custom_call_target="tpu_custom_call" | custom-call | flops 10616832000 | bytes 16777216 | tf_op jit(solution)/shard_map/local_maps/pallas_call | solution.py:327
  82.6 4.6 %collective-permute-start.3 = (f32[8,128,128]{2,1,0:T(8,128)S(1)}, f32[8,128,128]{2,1,0:T(8,128)S(1)}, u32[]{:S(2)}, u32[]{:S(2)}) collective-permute-start(f32[8,128,128]{2,1,0:T(8,128)S(1)} %convolution_add_fusion.5), channel_id=1, source_target_pairs={{0,4},{4,8},{8,12},{1,5},{5,9},{9,13},{2,6},{6,10},{10,14},{3,7},{... | collective-permute-start | bytes 1572872 | tf_op jit(solution)/shard_map/ppermute | solution.py:224
  87.2 8.3 %collective-permute-done.6 = f32[8,128,128]{2,1,0:T(8,128)S(1)} collective-permute-done((f32[8,128,128]{2,1,0:T(8,128)S(1)}, f32[8,128,128]{2,1,0:T(8,128)S(1)}, u32[]{:S(2)}, u32[]{:S(2)}) %collective-permute-start.6) | collective-permute-done | bytes 524320 | tf_op jit(solution)/shard_map/ppermute | solution.py:224
  98.5 4.8 %collective-permute-start.4 = (f32[8,128,128]{2,1,0:T(8,128)S(1)}, f32[8,128,128]{2,1,0:T(8,128)S(1)}, u32[]{:S(2)}, u32[]{:S(2)}) collective-permute-start(f32[8,128,128]{2,1,0:T(8,128)S(1)} %convolution_add_fusion.4), channel_id=1, source_target_pairs={{0,4},{4,8},{8,12},{1,5},{5,9},{9,13},{2,6},{6,10},{10,14},{3,7},{... | collective-permute-start | bytes 1572872 | tf_op jit(solution)/shard_map/ppermute | solution.py:224
  103.2 7.1 %collective-permute-done.7 = f32[8,128,128]{2,1,0:T(8,128)S(1)} collective-permute-done((f32[8,128,128]{2,1,0:T(8,128)S(1)}, f32[8,128,128]{2,1,0:T(8,128)S(1)}, u32[]{:S(2)}, u32[]{:S(2)}) %collective-permute-start.7) | collective-permute-done | bytes 524320 | tf_op jit(solution)/shard_map/ppermute | solution.py:224
  111.3 1.3 collective-permute-start.8
  113.3 4.6 %collective-permute-start.5 = (f32[8,128,128]{2,1,0:T(8,128)S(1)}, f32[8,128,128]{2,1,0:T(8,128)S(1)}, u32[]{:S(2)}, u32[]{:S(2)}) collective-permute-start(f32[8,128,128]{2,1,0:T(8,128)S(1)} %convolution_add_fusion.3), channel_id=1, source_target_pairs={{0,4},{4,8},{8,12},{1,5},{5,9},{9,13},{2,6},{6,10},{10,14},{3,7},{... | collective-permute-start | bytes 1572872 | tf_op jit(solution)/shard_map/ppermute | solution.py:224
  117.9 6.3 %collective-permute-done.8.leave_ref = f32[8,128,128]{2,1,0:T(8,128)S(1)} collective-permute-done((f32[8,128,128]{2,1,0:T(8,128)S(1)}, f32[8,128,128]{2,1,0:T(8,128)S(1)}, u32[]{:S(2)}, u32[]{:S(2)}) %collective-permute-start.8) | collective-permute-done | bytes 524320 | tf_op jit(solution)/shard_map/ppermute | solution.py:224
  124.2 1.8 collective-permute-done.5.enter_ref
  126.0 31.4 %results.1 = (bf16[128,1024]{1,0:T(8,128)(2,1)S(1)}, bf16[128,1024]{1,0:T(8,128)(2,1)S(1)}, bf16[128,1024]{1,0:T(8,128)(2,1)S(1)}, bf16[128,1024]{1,0:T(8,128)(2...) custom-call(f32[2]{0:T(128)S(1)} %fusion.20.retain_ref, ...), custom_call_target="tpu_custom_call" | custom-call | tf_op jit(solution)/shard_map/results/pallas_call | solution.py:344
  159.2 48.7 %all-gather.3.cloned.1.call-done = f32[544,1024]{1,0:T(8,128)} async-done(((f32[136,1024]{1,0:T(8,128)}), f32[544,1024]{1,0:T(8,128)}) %all-gather.3.cloned.1.call-update) | async-done | bytes 2228240 | tf_op jit(solution)/shard_map/all_gather | solution.py:365
  209.0 3.0 %fusion.1 = f32[512,1024]{1,0:T(8,128)S(1)} fusion(f32[128,512]{1,0:T(8,128)} %collective-permute-done, f32[4,136,1024]{2,1,0:T(8,128)} %bitcast.123, s32[]{:T(128)S(6)} %select_n.49), kind=kOutput, calls=%fused_computation.15 | convolution fusion | flops 805306368 | bytes 2883588 | tf_op jit(solution)/shard_map/dot_general | solution.py:368
  212.0 1.8 fusion.2
  213.9 1.8 fusion
  215.7 3.1 %add_add_fusion = f32[512,1024]{1,0:T(8,128)S(1)} fusion(f32[512,1024]{1,0:T(8,128)S(1)} %fusion, f32[512,1024]{1,0:T(8,128)S(1)} %fusion.2, f32[512,1024]{1,0:T(8,128)S(1)} %fusion.1, f32[128,512]{1,0:T(8,128)} %collective-permute-done.2, f32[4,136,1024]{2,1,0:T(8,128)S(1)} %bitcast.126, s32[]{:T(128)S(6)} %select_n.51), kind=kOutput, calls=%fused_computation.1 | convolution fusion | flops 806879232 | bytes 9175044 | tf_op jit(solution)/shard_map/dot_general | solution.py:368
  218.9 1.3 copy-done.2
  220.2 1.5 pad_maximum_fusion
  224.2 3.0 %fusion.27 = f32[128,2048]{1,0:T(8,128)S(1)} fusion(bf16[128,1024]{1,0:T(8,128)(2,1)S(1)} %get-tuple-element.38, bf16[1024,2048]{1,0:T(8,128)(2,1)} %param.16), kind=kOutput, calls=%fused_computation.62 | convolution fusion | flops 536870912 | bytes 5505024 | tf_op jit(solution)/shard_map/dot_general | solution.py:382
  228.0 1.5 collective-permute-start.9
  231.2 2.6 %maximum_bitcast_fusion = (bf16[1,128,3,8,128]{4,3,2,1,0:T(8,128)(2,1)}, bf16[1,128,3,8,128]{4,3,2,1,0:T(8,128)(2,1)}) fusion(bf16[128,1,8,128]{3,2,1,0:T(8,128)(2,1)} %bitcast.133, bf16[128,1,8,128]{3,2,1,0:T(8,128)(2,1)} %bitcast.132, bf16[128,1,8,128]{3,2,1,0:T(8,128)(2,1)S(1)} %bitcast.131, bf16[128,1,8,128]{3,2,1,0:T(8,128)(2,1)S(1)} %bitcast.130, ...), kind=kLoop, calls=%fused_computation.8 | loop fusion | flops 1572864 | bytes 3145728 | tf_op jit(solution)/shard_map/broadcast_in_dim | solution.py:387
  234.5 8.2 %collective-permute-done.9 = f32[128,1024]{1,0:T(8,128)} collective-permute-done((f32[128,1024]{1,0:T(8,128)}, f32[128,1024]{1,0:T(8,128)}, u32[]{:S(2)}, u32[]{:S(2)}) %collective-permute-start.9) | collective-permute-done | bytes 524320 | tf_op jit(solution)/shard_map/ppermute | solution.py:231
  242.7 1.8 fusion.5
  244.5 2.0 fusion.26
  246.5 1.5 slice.65
  (92 shorter events, 19.0 us)
Async XLA Ops:
  7.2 11.3 %copy-start.13 = (f32[1,8,128]{2,1,0:T(8,128)S(1)}, f32[1,8,128]{2,1,0:T(8,128)}, u32[]{:S(2)}) copy-start(f32[1,8,128]{2,1,0:T(8,128)} %param.13) | copy-start | bytes 12292
  7.2 11.4 %copy-start.15 = (f32[8]{0:T(128)S(1)}, f32[8]{0:T(128)}, u32[]{:S(2)}) copy-start(f32[8]{0:T(128)} %param.14) | copy-start | bytes 100
  7.2 200.7 %all-gather.3.cloned.1.call-start = ((), (), s32[]{:S(2)}) async-start(), calls=%async_computation | async-start | bytes 2785280 | tf_op jit(solution)/shard_map/all_gather | solution.py:365
  7.3 12.1 %copy-start.16 = (s32[1,8]{1,0:T(1,128)S(1)}, s32[1,8]{1,0:T(1,128)}, u32[]{:S(2)}) copy-start(s32[1,8]{1,0:T(1,128)} %param.15) | copy-start | bytes 100
  7.3 12.3 %copy-start.14 = (f32[1,8,3,128]{3,1,2,0:T(8,128)S(1)}, f32[1,8,3,128]{3,1,2,0:T(8,128)}, u32[]{:S(2)}) copy-start(f32[1,8,3,128]{3,1,2,0:T(8,128)} %param.12) | copy-start | bytes 36868
  11.5 68.1 %collective-permute-start = (f32[128,512]{1,0:T(8,128)}, f32[128,512]{1,0:T(8,128)}, u32[]{:S(2)}, u32[]{:S(2)}) collective-permute-start(f32[128,512]{1,0:T(8,128)} %get-tuple-element.94), channel_id=1, source_target_pairs={{0,4},{4,8},{8,12},{12,0},{1,5},{5,9},{9,13},{13,1},{2,6},{6,10},{... | collective-permute-start | bytes 786440 | tf_op jit(solution)/shard_map/ppermute | solution.py:231
  14.6 65.1 %collective-permute-start.1 = (f32[128,512]{1,0:T(8,128)}, f32[128,512]{1,0:T(8,128)S(1)}, u32[]{:S(2)}, u32[]{:S(2)}) collective-permute-start(f32[128,512]{1,0:T(8,128)} %get-tuple-element.93), channel_id=1, source_target_pairs={{0,8},{4,12},{8,0},{12,4},{1,9},{5,13},{9,1},{13,5},{2,10},{6,14},... | collective-permute-start | bytes 786440 | tf_op jit(solution)/shard_map/ppermute | solution.py:231
  17.2 62.6 %collective-permute-start.2 = (f32[128,512]{1,0:T(8,128)}, f32[128,512]{1,0:T(8,128)}, u32[]{:S(2)}, u32[]{:S(2)}) collective-permute-start(f32[128,512]{1,0:T(8,128)} %get-tuple-element.92), channel_id=1, source_target_pairs={{0,12},{4,0},{8,4},{12,8},{1,13},{5,1},{9,5},{13,9},{2,14},{6,2},{... | collective-permute-start | bytes 786440 | tf_op jit(solution)/shard_map/ppermute | solution.py:231
  19.8 0.8 copy-start.4
  19.9 3.7 %copy-start.7 = (bf16[1,128,2048]{2,1,0:T(8,128)(2,1)S(1)}, bf16[1,128,2048]{2,1,0:T(8,128)(2,1)}, u32[]{:S(2)}) copy-start(bf16[1,128,2048]{2,1,0:T(8,128)(2,1)} %param.17) | copy-start | bytes 1572868
  23.5 4.4 %copy-start = (bf16[128,3072]{1,0:T(8,128)(2,1)}, bf16[128,3072]{1,0:T(8,128)(2,1)S(1)}, u32[]{:S(2)}) copy-start(bf16[128,3072]{1,0:T(8,128)(2,1)S(1)} %reshape.71.v0.v1.v2) | copy-start | bytes 2359300
  23.6 4.0 %copy-start.12 = (bf16[1,128,8,128]{3,2,1,0:T(8,128)(2,1)S(1)}, bf16[1,128,8,128]{3,2,1,0:T(8,128)(2,1)}, u32[]{:S(2)}) copy-start(bf16[1,128,8,128]{3,2,1,0:T(8,128)(2,1)} %param.9) | copy-start | bytes 786436
  79.7 16.8 %copy-start.1 = (f32[8,2,128,128]{3,2,1,0:T(8,128)}, f32[8,2,128,128]{3,2,1,0:T(8,128)S(1)}, u32[]{:S(2)}) copy-start(f32[8,2,128,128]{3,2,1,0:T(8,128)S(1)} %get-tuple-element.31.map_ref) | copy-start | bytes 3145732
  79.7 16.8 %copy-start.10 = (f32[128,512]{1,0:T(8,128)}, f32[128,512]{1,0:T(8,128)S(1)}, u32[]{:S(2)}) copy-start(f32[128,512]{1,0:T(8,128)S(1)} %collective-permute-done.1) | copy-start | bytes 786436
  80.7 14.7 %collective-permute-start.6 = (f32[8,128,128]{2,1,0:T(8,128)S(1)}, f32[8,128,128]{2,1,0:T(8,128)S(1)}, u32[]{:S(2)}, u32[]{:S(2)}) collective-permute-start(f32[8,128,128]{2,1,0:T(8,128)S(1)} %convolution_add_fusion.2), channel_id=1, source_target_pairs={{4,0},{8,4},{12,8},{5,1},{9,5},{13,9},{6,2},{10,6},{14,10},{7,3},{... | collective-permute-start | bytes 1572872 | tf_op jit(solution)/shard_map/ppermute | solution.py:224
  82.6 15.2 %collective-permute-start.3 = (f32[8,128,128]{2,1,0:T(8,128)S(1)}, f32[8,128,128]{2,1,0:T(8,128)S(1)}, u32[]{:S(2)}, u32[]{:S(2)}) collective-permute-start(f32[8,128,128]{2,1,0:T(8,128)S(1)} %convolution_add_fusion.5), channel_id=1, source_target_pairs={{0,4},{4,8},{8,12},{1,5},{5,9},{9,13},{2,6},{6,10},{10,14},{3,7},{... | collective-permute-start | bytes 1572872 | tf_op jit(solution)/shard_map/ppermute | solution.py:224
  96.5 13.8 %collective-permute-start.7 = (f32[8,128,128]{2,1,0:T(8,128)S(1)}, f32[8,128,128]{2,1,0:T(8,128)S(1)}, u32[]{:S(2)}, u32[]{:S(2)}) collective-permute-start(f32[8,128,128]{2,1,0:T(8,128)S(1)} %convolution_add_fusion.1), channel_id=1, source_target_pairs={{4,0},{8,4},{12,8},{5,1},{9,5},{13,9},{6,2},{10,6},{14,10},{7,3},{... | collective-permute-start | bytes 1572872 | tf_op jit(solution)/shard_map/ppermute | solution.py:224
  98.5 14.1 %collective-permute-start.4 = (f32[8,128,128]{2,1,0:T(8,128)S(1)}, f32[8,128,128]{2,1,0:T(8,128)S(1)}, u32[]{:S(2)}, u32[]{:S(2)}) collective-permute-start(f32[8,128,128]{2,1,0:T(8,128)S(1)} %convolution_add_fusion.4), channel_id=1, source_target_pairs={{0,4},{4,8},{8,12},{1,5},{5,9},{9,13},{2,6},{6,10},{10,14},{3,7},{... | collective-permute-start | bytes 1572872 | tf_op jit(solution)/shard_map/ppermute | solution.py:224
  111.3 12.9 %collective-permute-start.8 = (f32[8,128,128]{2,1,0:T(8,128)S(1)}, f32[8,128,128]{2,1,0:T(8,128)S(1)}, u32[]{:S(2)}, u32[]{:S(2)}) collective-permute-start(f32[8,128,128]{2,1,0:T(8,128)S(1)} %convolution_add_fusion), channel_id=1, source_target_pairs={{4,0},{8,4},{12,8},{5,1},{9,5},{13,9},{6,2},{10,6},{14,10},{7,3},{... | collective-permute-start | bytes 1572872 | tf_op jit(solution)/shard_map/ppermute | solution.py:224
  113.3 12.8 %collective-permute-start.5 = (f32[8,128,128]{2,1,0:T(8,128)S(1)}, f32[8,128,128]{2,1,0:T(8,128)S(1)}, u32[]{:S(2)}, u32[]{:S(2)}) collective-permute-start(f32[8,128,128]{2,1,0:T(8,128)S(1)} %convolution_add_fusion.3), channel_id=1, source_target_pairs={{0,4},{4,8},{8,12},{1,5},{5,9},{9,13},{2,6},{6,10},{10,14},{3,7},{... | collective-permute-start | bytes 1572872 | tf_op jit(solution)/shard_map/ppermute | solution.py:224
  158.3 53.6 %copy-start.8 = (f32[128,512]{1,0:T(8,128)S(1)}, f32[128,512]{1,0:T(8,128)}, u32[]{:S(2)}) copy-start(f32[128,512]{1,0:T(8,128)} %get-tuple-element.48) | copy-start | bytes 786436
  207.9 4.1 %copy-start.6 = (f32[544,1024]{1,0:T(8,128)S(1)}, f32[544,1024]{1,0:T(8,128)}, u32[]{:S(2)}) copy-start(f32[544,1024]{1,0:T(8,128)} %all-gather.3.cloned.1.call-done) | copy-start | bytes 6684676
  212.0 1.9 copy-start.11
  218.9 1.3 copy-start.2
  221.7 22.8 %collective-permute-start.10 = (f32[520,1024]{1,0:T(8,128)}, f32[520,1024]{1,0:T(8,128)}, u32[]{:S(2)}, u32[]{:S(2)}) collective-permute-start(f32[520,1024]{1,0:T(8,128)} %pad_maximum_fusion), channel_id=1, source_target_pairs={{0,1},{1,0},{2,3},{3,2},{4,5},{5,4},{6,7},{7,6},{8,9},{9,8},{10,11... | collective-permute-start | bytes 6389768 | tf_op jit(solution)/shard_map/ppermute | solution.py:231
  224.2 5.3 %copy-start.5 = (f32[1,8,3,128]{2,3,1,0:T(8,128)S(1)}, f32[1,8,3,128]{2,3,1,0:T(8,128)}, u32[]{:S(2)}) copy-start(f32[1,8,3,128]{2,3,1,0:T(8,128)} %copy-done.4) | copy-start | bytes 36868
  227.2 4.0 %copy-start.9 = (bf16[16,8,8,128]{3,2,1,0:T(8,128)(2,1)S(1)}, bf16[16,8,8,128]{3,2,1,0:T(8,128)(2,1)}, u32[]{:S(2)}) copy-start(bf16[16,8,8,128]{3,2,1,0:T(8,128)(2,1)} %copy.121) | copy-start | bytes 786436
  228.0 14.7 %collective-permute-start.9 = (f32[128,1024]{1,0:T(8,128)}, f32[128,1024]{1,0:T(8,128)}, u32[]{:S(2)}, u32[]{:S(2)}) collective-permute-start(f32[128,1024]{1,0:T(8,128)} %constant_dynamic-slice_fusion), channel_id=1, source_target_pairs={{0,2},{2,0},{1,3},{3,1},{4,6},{6,4},{5,7},{7,5},{8,10},{10,8},{9,1... | collective-permute-start | bytes 1572872 | tf_op jit(solution)/shard_map/ppermute | solution.py:231
  231.2 13.3 %copy-start.3 = (f32[512,1024]{1,0:T(8,128)S(1)}, f32[512,1024]{1,0:T(8,128)}, u32[]{:S(2)}) copy-start(f32[512,1024]{1,0:T(8,128)} %copy-done.2) | copy-start | bytes 6291460
Sparse Core Ops, SparseCore 0:
  159.3 48.5 all-gather.2
